TPU v7x, 32 devices: a whole 2x2x4 slice. The times are simulated.
32 devices in a mesh: pitch: 4 (over x, core), span: 8 (over z, y).
Axes of the slice: x: 2, y: 2, z: 4, core: 2. Of those that a mesh axis runs over, the one named last changes fastest.
Arguments:
- residual: float32 [5, 4, 64, 1024], P(None, None, 'span', 'pitch'), may hold values from -0.6 to 0.6
- inverse_diagonal: float32 [5, 5, 4, 64, 1024], P(None, None, None, 'span', 'pitch'), may hold values from -0.1 to 1, as said below
- prior_increment: float32 [5, 4, 64, 1024], P(None, None, 'span', 'pitch'), may hold values from -3 to 3
- coupling: float32 [6, 5, 5], replicated, may hold values from -1 to 1
- characteristic: float32 [2, 2, 512, 5, 5], replicated, may hold values from -6 to 6
- cutoffs: int32 [2], replicated, may hold values from 128 to 512
Outputs:
- update: float32 [5, 4, 64, 1024], P(None, None, 'span', 'pitch')
Inputs may be any that keep to these rules, and one draw needn't show every extreme that they name: `inverse_diagonal`: each cell's block is dominated by its diagonal; the sweeps' recurrences are stable.
All inputs are finite; a program needn't handle non-finite values.
Results may differ from a plain program's by a relative error of at most 0.0003.
Values sent between devices are 32-bit elements; how exact they have to be, the bound alone decides.
A program may use at most 64 MiB of HBM per device.

v0:
```python
import jax
import jax.numpy as jnp
from jax import lax
from jax.sharding import PartitionSpec as P

NP = 1024
HARMONICS = 512


highest = lax.Precision.HIGHEST


def extended(array, sides, width):
    for axis, dim in sides:
        size, length = (lax.axis_size(axis), array.shape[dim])
        up = [(i, (i + 1) % size) for i in range(size)]
        down = [(j, i) for i, j in up]
        last = lax.slice_in_dim(array, length - width, length, axis=dim)
        initial = lax.slice_in_dim(array, 0, width, axis=dim)
        before = lax.ppermute(last, axis, up)
        after = lax.ppermute(initial, axis, down)
        array = jnp.concatenate([before, array, after], axis=dim)
    return array


def passed_along(value, axis, steps):
    count = lax.axis_size(axis)
    initial, last = (max(0, -steps), min(count, count - steps))
    return lax.ppermute(value, axis, [(source, source + steps) for source in range(initial, last)])


def angle_tables(pitch_index, harmonic_index, points):
    product = pitch_index[:, None] * harmonic_index[None, :] % points
    angles = product.astype(jnp.float32) * (2.0 * jnp.pi / points)
    return (jnp.cos(angles), jnp.sin(angles))


def forward_dft(spanwise_slices, cosine, sine):
    flat = spanwise_slices.reshape(-1, spanwise_slices.shape[-1])
    shape = spanwise_slices.shape[:-1] + (cosine.shape[1],)
    real_part = jnp.dot(flat, cosine, precision=highest).reshape(shape)
    imag_part = -jnp.dot(flat, sine, precision=highest).reshape(shape)
    return (real_part, imag_part)


def contract(matrix, spectrum):
    return jnp.einsum("pkij,pjrk->pirk", matrix, spectrum, precision=highest)


def apply_harmonics(real_part, imag_part, characteristic, cutoffs, first_harmonic, points):
    char_real = characteristic[:, 0]
    char_imag = characteristic[:, 1]
    result_real_component = contract(char_real, real_part) - contract(char_imag, imag_part)
    out_imag = contract(char_real, imag_part) + contract(char_imag, real_part)
    harmonic = first_harmonic + jnp.arange(real_part.shape[-1], dtype=jnp.int32)
    kept = (harmonic[None, :] < cutoffs[:, None]).astype(jnp.float32)
    weight = jnp.where(harmonic == 0, 1.0, 2.0).astype(jnp.float32) / points
    factor = (kept * weight[None, :])[:, None, None, :]
    return (result_real_component * factor, out_imag * factor)


def inverse_dft(result_real_component, out_imag, cosine, sine):
    shape = result_real_component.shape[:-1] + (cosine.shape[0],)
    flat_real = result_real_component.reshape(-1, result_real_component.shape[-1])
    flat_imag = out_imag.reshape(-1, out_imag.shape[-1])
    result = jnp.dot(flat_real, cosine.T, precision=highest) - jnp.dot(
        flat_imag, sine.T, precision=highest
    )
    return result.reshape(shape)


def mix_field(matrix, field):
    return jnp.einsum("ij,jarp->iarp", matrix, field, precision=highest)


def mix_vector(matrix, vector):
    return jnp.einsum("ij,jap->iap", matrix, vector, precision=highest)


def apply_block(block, vector):
    return jnp.einsum("ijap,jap->iap", block, vector, precision=highest)


def local_maps(inverse_diagonal, sources, matrix, descending):
    variables = inverse_diagonal.shape[0]
    axial_cell_count = inverse_diagonal.shape[2]
    radial = inverse_diagonal.shape[3]
    pitch_cells = inverse_diagonal.shape[4]
    identity = jnp.broadcast_to(
        jnp.eye(variables, dtype=jnp.float32)[:, :, None, None],
        (variables, variables, axial_cell_count, pitch_cells),
    )
    zero_vector = jnp.zeros((variables, axial_cell_count, pitch_cells), jnp.float32)

    def compose(step_index, carry):
        maps, offset = carry
        row_index = radial - 1 - step_index if descending else step_index
        block = lax.dynamic_index_in_dim(inverse_diagonal, row_index, 3, keepdims=False)
        rhs_row = lax.dynamic_index_in_dim(sources, row_index, 2, keepdims=False)
        factor = -jnp.einsum("ijap,jk->ikap", block, matrix, precision=highest)
        inject = rhs_row if descending else apply_block(block, rhs_row)
        maps = jnp.einsum("ijap,jkap->ikap", factor, maps, precision=highest)
        return (maps, apply_block(factor, offset) + inject)

    return (lax.fori_loop(0, radial, compose, (identity, zero_vector)), (identity, zero_vector))


def sweep_rows(inverse_diagonal, sources, matrix, incoming, descending):
    radial = inverse_diagonal.shape[3]

    def advance(step_index, carry):
        previous, buffer = carry
        row_index = radial - 1 - step_index if descending else step_index
        block = lax.dynamic_index_in_dim(inverse_diagonal, row_index, 3, keepdims=False)
        rhs_row = lax.dynamic_index_in_dim(sources, row_index, 2, keepdims=False)
        if descending:
            current = rhs_row - apply_block(block, mix_vector(matrix, previous))
        else:
            current = apply_block(block, rhs_row - mix_vector(matrix, previous))
        buffer = lax.dynamic_update_index_in_dim(buffer, current, row_index, 2)
        return (current, buffer)

    _, result = lax.fori_loop(0, radial, advance, (incoming, jnp.zeros_like(sources)))
    return result


def body(residual, inverse_diagonal, prior_increment, coupling, characteristic, cutoffs):
    spanwise_slices = jnp.stack([residual[:, 0], residual[:, -1]])
    pitch_cells = residual.shape[3]
    harmonic_index = jnp.arange(HARMONICS, dtype=jnp.int32)
    own_faces = lax.axis_index("pitch") * pitch_cells + jnp.arange(pitch_cells, dtype=jnp.int32)
    cosine, sine = angle_tables(own_faces, harmonic_index, NP)
    real_part, imag_part = forward_dft(spanwise_slices, cosine, sine)
    real_part, imag_part = (
        lax.psum_scatter(real_part, "pitch", scatter_dimension=3, tiled=True),
        lax.psum_scatter(imag_part, "pitch", scatter_dimension=3, tiled=True),
    )
    own_count = HARMONICS // lax.axis_size("pitch")
    first_harmonic = lax.axis_index("pitch") * own_count
    own_matrices = lax.dynamic_slice_in_dim(characteristic, first_harmonic, own_count, 2)
    result_real_component, out_imag = apply_harmonics(
        real_part, imag_part, own_matrices, cutoffs, first_harmonic, NP
    )
    own_harmonics = first_harmonic + jnp.arange(own_count, dtype=jnp.int32)
    all_cosine, all_sine = angle_tables(jnp.arange(NP, dtype=jnp.int32), own_harmonics, NP)
    partial_terms = inverse_dft(result_real_component, out_imag, all_cosine, all_sine)
    correction = lax.psum_scatter(partial_terms, "pitch", scatter_dimension=3, tiled=True)
    corrected = residual.at[:, 0].add(correction[0]).at[:, -1].add(correction[1])
    padded = extended(prior_increment, (("pitch", 3),), 1)
    axial_pad = jnp.pad(prior_increment, ((0, 0), (1, 1), (0, 0), (0, 0)))
    source = (
        corrected
        - mix_field(coupling[2], padded[..., :-2])
        - mix_field(coupling[3], padded[..., 2:])
    )
    source = (
        source
        - mix_field(coupling[4], axial_pad[:, :-2])
        - mix_field(coupling[5], axial_pad[:, 2:])
    )
    (forward_maps, forward_offset), identity_pair = local_maps(
        inverse_diagonal, source, coupling[0], False
    )

    def forward_link(step_index, incoming):
        outgoing = apply_block(forward_maps, incoming) + forward_offset
        return passed_along(outgoing, "span", 1)

    forward_in = lax.fori_loop(0, lax.axis_size("span") - 1, forward_link, identity_pair[1])
    star = sweep_rows(inverse_diagonal, source, coupling[0], forward_in, False)
    (backward_maps, backward_offset), identity_pair = local_maps(
        inverse_diagonal, star, coupling[1], True
    )

    def backward_link(step_index, incoming):
        outgoing = apply_block(backward_maps, incoming) + backward_offset
        return passed_along(outgoing, "span", -1)

    backward_in = lax.fori_loop(0, lax.axis_size("span") - 1, backward_link, identity_pair[1])
    return sweep_rows(inverse_diagonal, star, coupling[1], backward_in, True)


def solution(mesh):
    in_specs = (
        P(None, None, "span", "pitch"),
        P(None, None, None, "span", "pitch"),
        P(None, None, "span", "pitch"),
        P(),
        P(),
        P(),
    )
    out_specs = P(None, None, "span", "pitch")
    return jax.shard_map(body, mesh=mesh, in_specs=in_specs, out_specs=out_specs, check_vma=False)
```

profile of v0, /device:TPU:0, one launch (start us, length us, event | category | flops | bytes accessed | tf_op | source)
XLA Modules:
  0.0 542.4 jit_solution(13137576944903437122)
XLA Ops:
  23.5 9.6 %reduce-scatter.4.cloned.1.call-done = f32[2,5,8,128]{3,2,1,0:T(8,128)} async-done(((f32[2,5,8,512]{3,2,1,0:T(8,128)}), f32[2,5,8,128]{3,2,1,0:T(8,128)}) %reduce-scatter.4.cloned.1.call-update) | async-done | bytes 40976 | tf_op jit(solution)/shard_map/reduce_scatter | solution.py:135
  37.1 18.2 %reduce-scatter.6.cloned.1.call-done = f32[2,5,8,128]{3,2,1,0:T(8,128)} async-done(((f32[2,5,8,512]{3,2,1,0:T(8,128)}), f32[2,5,8,128]{3,2,1,0:T(8,128)}) %reduce-scatter.6.cloned.1.call-update) | async-done | bytes 40976 | tf_op jit(solution)/shard_map/reduce_scatter | solution.py:136
  85.8 16.4 %reduce-scatter.8.cloned.1.call-done = f32[2,5,8,256]{3,2,1,0:T(8,128)} async-done(((f32[2,5,8,1024]{3,2,1,0:T(8,128)}), f32[2,5,8,256]{3,2,1,0:T(8,128)}) %reduce-scatter.8.cloned.1.call-update) | async-done | bytes 81936 | tf_op jit(solution)/shard_map/reduce_scatter | solution.py:147
  108.5 183.9 %while.87 = (s32[]{:T(128)}, f32[5,5,4,256]{1,0,3,2:T(8,128)}, f32[5,4,256]{0,2,1:T(8,128)S(1)}, f32[5,5,4,8,256]{4,1,2,0,3:T(8,128)S(1)}, f32[5,5]{0,1:T(8,128)S(1)}, /*index=5*/f32[5,4,8,256]{3,2,1,0:T(8,128)S(1)}, s32[]{:T(128)}) while((s32[]{:T(128)}, f32[5,5,4,256]{1,0,3,2:T(8,128)}, f32[5,4,256]{0,2,1:T(8,128)S(1)}, ...), condition=%wide.region_4.5_spmd, body=%wide.region_3.4_spmd.sunk | while | flops 3456002 | bytes 2318481 | solution.py:105
  112.1 8.9 %fusion.134 = f32[4,256,1,5]{3,2,1,0:T(1,128)S(1)} fusion(f32[5,5,4,256]{1,0,3,2:T(8,128)} %copy.215, f32[5,4,256,1]{0,3,2,1:T(1,128)S(1)} %bitcast.282), kind=kOutput, calls=%fused_computation.146.clone.1 | convolution fusion | flops 307200 | bytes 143360 | tf_op jit(solution)/shard_map/while/body/eval_jaxpr/ijap,jap->iap/dot_general | solution.py:81
  135.1 8.9 %fusion.134 = f32[4,256,1,5]{3,2,1,0:T(1,128)S(1)} fusion(f32[5,5,4,256]{1,0,3,2:T(8,128)} %copy.215, f32[5,4,256,1]{0,3,2,1:T(1,128)S(1)} %bitcast.282), kind=kOutput, calls=%fused_computation.146.clone.1 | convolution fusion | flops 307200 | bytes 143360 | tf_op jit(solution)/shard_map/while/body/eval_jaxpr/ijap,jap->iap/dot_general | solution.py:81
  146.3 8.4 %convolution_bitcast_fusion.4 = f32[5,5,4,256]{1,0,3,2:T(8,128)} fusion(f32[5,5,4,256]{1,0,3,2:T(8,128)S(1)} %copy-done, f32[5,5,4,256]{1,0,3,2:T(8,128)S(1)} %copy.285), kind=kOutput, calls=%fused_computation.clone.1 | convolution fusion | flops 1536000 | bytes 307200 | tf_op jit(solution)/shard_map/while/body/eval_jaxpr/ijap,jkap->ikap/dot_general | solution.py:102
  158.0 8.9 %fusion.134 = f32[4,256,1,5]{3,2,1,0:T(1,128)S(1)} fusion(f32[5,5,4,256]{1,0,3,2:T(8,128)} %copy.215, f32[5,4,256,1]{0,3,2,1:T(1,128)S(1)} %bitcast.282), kind=kOutput, calls=%fused_computation.146.clone.1 | convolution fusion | flops 307200 | bytes 143360 | tf_op jit(solution)/shard_map/while/body/eval_jaxpr/ijap,jap->iap/dot_general | solution.py:81
  169.2 8.4 %convolution_bitcast_fusion.4 = f32[5,5,4,256]{1,0,3,2:T(8,128)} fusion(f32[5,5,4,256]{1,0,3,2:T(8,128)S(1)} %copy-done, f32[5,5,4,256]{1,0,3,2:T(8,128)S(1)} %copy.285), kind=kOutput, calls=%fused_computation.clone.1 | convolution fusion | flops 1536000 | bytes 307200 | tf_op jit(solution)/shard_map/while/body/eval_jaxpr/ijap,jkap->ikap/dot_general | solution.py:102
  181.0 8.9 %fusion.134 = f32[4,256,1,5]{3,2,1,0:T(1,128)S(1)} fusion(f32[5,5,4,256]{1,0,3,2:T(8,128)} %copy.215, f32[5,4,256,1]{0,3,2,1:T(1,128)S(1)} %bitcast.282), kind=kOutput, calls=%fused_computation.146.clone.1 | convolution fusion | flops 307200 | bytes 143360 | tf_op jit(solution)/shard_map/while/body/eval_jaxpr/ijap,jap->iap/dot_general | solution.py:81
  192.2 8.4 %convolution_bitcast_fusion.4 = f32[5,5,4,256]{1,0,3,2:T(8,128)} fusion(f32[5,5,4,256]{1,0,3,2:T(8,128)S(1)} %copy-done, f32[5,5,4,256]{1,0,3,2:T(8,128)S(1)} %copy.285), kind=kOutput, calls=%fused_computation.clone.1 | convolution fusion | flops 1536000 | bytes 307200 | tf_op jit(solution)/shard_map/while/body/eval_jaxpr/ijap,jkap->ikap/dot_general | solution.py:102
  203.9 8.9 %fusion.134 = f32[4,256,1,5]{3,2,1,0:T(1,128)S(1)} fusion(f32[5,5,4,256]{1,0,3,2:T(8,128)} %copy.215, f32[5,4,256,1]{0,3,2,1:T(1,128)S(1)} %bitcast.282), kind=kOutput, calls=%fused_computation.146.clone.1 | convolution fusion | flops 307200 | bytes 143360 | tf_op jit(solution)/shard_map/while/body/eval_jaxpr/ijap,jap->iap/dot_general | solution.py:81
  215.1 8.4 %convolution_bitcast_fusion.4 = f32[5,5,4,256]{1,0,3,2:T(8,128)} fusion(f32[5,5,4,256]{1,0,3,2:T(8,128)S(1)} %copy-done, f32[5,5,4,256]{1,0,3,2:T(8,128)S(1)} %copy.285), kind=kOutput, calls=%fused_computation.clone.1 | convolution fusion | flops 1536000 | bytes 307200 | tf_op jit(solution)/shard_map/while/body/eval_jaxpr/ijap,jkap->ikap/dot_general | solution.py:102
  226.9 8.9 %fusion.134 = f32[4,256,1,5]{3,2,1,0:T(1,128)S(1)} fusion(f32[5,5,4,256]{1,0,3,2:T(8,128)} %copy.215, f32[5,4,256,1]{0,3,2,1:T(1,128)S(1)} %bitcast.282), kind=kOutput, calls=%fused_computation.146.clone.1 | convolution fusion | flops 307200 | bytes 143360 | tf_op jit(solution)/shard_map/while/body/eval_jaxpr/ijap,jap->iap/dot_general | solution.py:81
  238.1 8.4 %convolution_bitcast_fusion.4 = f32[5,5,4,256]{1,0,3,2:T(8,128)} fusion(f32[5,5,4,256]{1,0,3,2:T(8,128)S(1)} %copy-done, f32[5,5,4,256]{1,0,3,2:T(8,128)S(1)} %copy.285), kind=kOutput, calls=%fused_computation.clone.1 | convolution fusion | flops 1536000 | bytes 307200 | tf_op jit(solution)/shard_map/while/body/eval_jaxpr/ijap,jkap->ikap/dot_general | solution.py:102
  249.8 8.9 %fusion.134 = f32[4,256,1,5]{3,2,1,0:T(1,128)S(1)} fusion(f32[5,5,4,256]{1,0,3,2:T(8,128)} %copy.215, f32[5,4,256,1]{0,3,2,1:T(1,128)S(1)} %bitcast.282), kind=kOutput, calls=%fused_computation.146.clone.1 | convolution fusion | flops 307200 | bytes 143360 | tf_op jit(solution)/shard_map/while/body/eval_jaxpr/ijap,jap->iap/dot_general | solution.py:81
  261.0 8.4 %convolution_bitcast_fusion.4 = f32[5,5,4,256]{1,0,3,2:T(8,128)} fusion(f32[5,5,4,256]{1,0,3,2:T(8,128)S(1)} %copy-done, f32[5,5,4,256]{1,0,3,2:T(8,128)S(1)} %copy.285), kind=kOutput, calls=%fused_computation.clone.1 | convolution fusion | flops 1536000 | bytes 307200 | tf_op jit(solution)/shard_map/while/body/eval_jaxpr/ijap,jkap->ikap/dot_general | solution.py:102
  272.8 8.9 %fusion.134 = f32[4,256,1,5]{3,2,1,0:T(1,128)S(1)} fusion(f32[5,5,4,256]{1,0,3,2:T(8,128)} %copy.215, f32[5,4,256,1]{0,3,2,1:T(1,128)S(1)} %bitcast.282), kind=kOutput, calls=%fused_computation.146.clone.1 | convolution fusion | flops 307200 | bytes 143360 | tf_op jit(solution)/shard_map/while/body/eval_jaxpr/ijap,jap->iap/dot_general | solution.py:81
  284.0 8.4 %convolution_bitcast_fusion.4 = f32[5,5,4,256]{1,0,3,2:T(8,128)} fusion(f32[5,5,4,256]{1,0,3,2:T(8,128)S(1)} %copy-done, f32[5,5,4,256]{1,0,3,2:T(8,128)S(1)} %copy.285), kind=kOutput, calls=%fused_computation.clone.1 | convolution fusion | flops 1536000 | bytes 307200 | tf_op jit(solution)/shard_map/while/body/eval_jaxpr/ijap,jkap->ikap/dot_general | solution.py:102
  295.2 42.9 %while.88 = (s32[]{:T(128)}, f32[5,4,256]{2,1,0:T(4,128)S(1)}, f32[5,5,4,256]{3,2,1,0:T(4,128)S(1)}, f32[5,4,256]{2,1,0:T(4,128)S(1)}, s32[]{:T(128)}) while((s32[]{:T(128)}, f32[5,4,256]{2,1,0:T(4,128)S(1)}, f32[5,5,4,256]{3,2,1,0:T(4,128)S(1)}, f32[5,4,256]{2,1,0:T(4,128)S(1)}, s32[]{:T(128)}) %tuple.178), condition=%wide.region_6.7_spmd, body=%wide.region_5.6_spmd.sunk | while | flops 51202 | bytes 286821 | solution.py:169
  338.1 13.0 %while.89 = (s32[]{:T(128)}, f32[5,4,256]{2,1,0:T(4,128)S(1)}, f32[5,4,8,256]{3,2,1,0:T(8,128)S(1)}, f32[5,4,8,256]{3,2,1,0:T(8,128)S(1)}, f32[5,5]{1,0:T(8,128)...) while((s32[]{:T(128)}, f32[5,4,256]{2,1,0:T(4,128)S(1)}, f32[5,4,8,256]{3,2,1,0:T(8,128)S(1)}, ...), condition=%wide.region_8.9_spmd, body=%wide.region_7.8_spmd.sunk | while | flops 358402 | bytes 573637 | solution.py:123
  353.4 118.9 %while.92 = (s32[]{:T(128)}, f32[5,5,4,256]{1,0,3,2:T(8,128)}, f32[5,4,256]{2,1,0:T(4,128)S(1)}, f32[5,5,4,8,256]{4,1,2,0,3:T(8,128)S(1)}, f32[5,5]{0,1:T(8,128)...) while((s32[]{:T(128)}, f32[5,5,4,256]{1,0,3,2:T(8,128)}, ...), condition=%wide.region_10.11_spmd.clone, body=%wide.region_9.10_spmd.clone.sunk | while | flops 3153927 | bytes 1634497 | solution.py:105
  475.0 47.0 %while.90 = (s32[]{:T(128)}, f32[5,4,256]{2,1,0:T(4,128)S(1)}, f32[5,5,4,256]{3,2,1,0:T(4,128)S(1)}, f32[5,4,256]{2,1,0:T(4,128)S(1)}, s32[]{:T(128)}) while((s32[]{:T(128)}, f32[5,4,256]{2,1,0:T(4,128)S(1)}, f32[5,5,4,256]{3,2,1,0:T(4,128)S(1)}, f32[5,4,256]{2,1,0:T(4,128)S(1)}, s32[]{:T(128)}) %tuple.187), condition=%wide.region_12.13_spmd, body=%wide.region_11.12_spmd.sunk | while | flops 51202 | bytes 286821 | solution.py:179
  522.0 13.2 %while.91 = (s32[]{:T(128)}, f32[5,4,256]{2,1,0:T(4,128)S(1)}, f32[5,4,8,256]{3,2,1,0:T(8,128)S(1)}, f32[5,4,8,256]{3,2,1,0:T(8,128)S(1)}, f32[5,5]{1,0:T(8,128)...) while((s32[]{:T(128)}, f32[5,4,256]{2,1,0:T(4,128)S(1)}, ...), condition=%wide.region_14.15_spmd, body=%wide.region_13.14_spmd.sunk | while | flops 358406 | bytes 614659 | solution.py:123
  (439 shorter events, 352.2 us)
Async XLA Ops:
  6.5 12.2 %copy-start.5 = (f32[5,4,8,256]{3,2,1,0:T(8,128)S(1)}, f32[5,4,8,256]{3,2,1,0:T(8,128)}, u32[]{:S(2)}) copy-start(f32[5,4,8,256]{3,2,1,0:T(8,128)} %param.24) | copy-start | bytes 491524
  6.5 11.6 %copy-start.10 = (f32[6,5,5]{2,0,1:T(8,128)S(1)}, f32[6,5,5]{2,0,1:T(8,128)}, u32[]{:S(2)}) copy-start(f32[6,5,5]{2,0,1:T(8,128)} %param.25) | copy-start | bytes 1804
  6.5 15.4 %copy-start.11 = (s32[2]{0:T(128)S(1)}, s32[2]{0:T(128)}, u32[]{:S(2)}) copy-start(s32[2]{0:T(128)} %param.27) | copy-start | bytes 28
  6.5 26.6 %reduce-scatter.4.cloned.1.call-start = ((), (), s32[]{:S(2)}) async-start(), calls=%async_computation.3 | async-start | bytes 204800 | tf_op jit(solution)/shard_map/reduce_scatter | solution.py:135
  10.5 44.8 %reduce-scatter.6.cloned.1.call-start = ((), (), s32[]{:S(2)}) async-start(), calls=%async_computation.4 | async-start | bytes 204800 | tf_op jit(solution)/shard_map/reduce_scatter | solution.py:136
  12.3 71.6 %collective-permute-start.3 = (f32[5,4,8,1]{3,0,2,1:T(8,128)}, f32[5,4,8,1]{3,0,2,1:T(8,128)}, u32[]{:S(2)}, u32[]{:S(2)}) collective-permute-start(f32[5,4,8,1]{3,0,2,1:T(8,128)} %get-tuple-element.761), channel_id=1, source_target_pairs={{8,0},{16,8},{24,16},{0,24},{9,1},{17,9},{25,17},{1,25},{10,2},{18... | collective-permute-start | bytes 1928 | tf_op jit(solution)/shard_map/ppermute | solution.py:21
  14.7 70.6 %collective-permute-start.2 = (f32[5,4,8,1]{3,0,2,1:T(8,128)}, f32[5,4,8,1]{3,0,2,1:T(8,128)S(1)}, u32[]{:S(2)}, u32[]{:S(2)}) collective-permute-start(f32[5,4,8,1]{3,0,2,1:T(8,128)} %get-tuple-element.760), channel_id=1, source_target_pairs={{0,8},{8,16},{16,24},{24,0},{1,9},{9,17},{17,25},{25,1},{2,10},{10... | collective-permute-start | bytes 1928 | tf_op jit(solution)/shard_map/ppermute | solution.py:20
  17.9 84.4 %reduce-scatter.8.cloned.1.call-start = ((), (), s32[]{:S(2)}) async-start(), calls=%async_computation.5 | async-start | bytes 409600 | tf_op jit(solution)/shard_map/reduce_scatter | solution.py:147
  75.7 29.4 %copy-start.6 = (f32[4,8,256,5]{2,3,1,0:T(8,128)S(1)}, f32[4,8,256,5]{2,3,1,0:T(8,128)}, u32[]{:S(2)}) copy-start(f32[4,8,256,5]{2,3,1,0:T(8,128)} %fusion.59) | copy-start | bytes 491524
  75.7 29.4 %copy-start.7 = (f32[4,8,256,5]{2,3,1,0:T(8,128)S(1)}, f32[4,8,256,5]{2,3,1,0:T(8,128)}, u32[]{:S(2)}) copy-start(f32[4,8,256,5]{2,3,1,0:T(8,128)} %fusion.61) | copy-start | bytes 491524
  295.3 4.8 collective-permute-start
  300.2 5.7 %collective-permute-start = (f32[5,4,256]{2,1,0:T(4,128)S(1)}, f32[5,4,256]{2,1,0:T(4,128)S(1)}, u32[]{:S(2)}, u32[]{:S(2)}) collective-permute-start(f32[5,4,256]{2,1,0:T(4,128)S(1)} %bitcast_add_fusion.6), channel_id=1, source_target_pairs={{0,1},{1,2},{2,3},{3,4},{4,5},{5,6},{6,7},{8,9},{9,10},{10,11},{11... | collective-permute-start | bytes 61448 | tf_op jit(solution)/shard_map/while/body/eval_jaxpr/ppermute | solution.py:29
  305.9 5.8 %collective-permute-start = (f32[5,4,256]{2,1,0:T(4,128)S(1)}, f32[5,4,256]{2,1,0:T(4,128)S(1)}, u32[]{:S(2)}, u32[]{:S(2)}) collective-permute-start(f32[5,4,256]{2,1,0:T(4,128)S(1)} %bitcast_add_fusion.6), channel_id=1, source_target_pairs={{0,1},{1,2},{2,3},{3,4},{4,5},{5,6},{6,7},{8,9},{9,10},{10,11},{11... | collective-permute-start | bytes 61448 | tf_op jit(solution)/shard_map/while/body/eval_jaxpr/ppermute | solution.py:29
  311.7 6.6 %collective-permute-start = (f32[5,4,256]{2,1,0:T(4,128)S(1)}, f32[5,4,256]{2,1,0:T(4,128)S(1)}, u32[]{:S(2)}, u32[]{:S(2)}) collective-permute-start(f32[5,4,256]{2,1,0:T(4,128)S(1)} %bitcast_add_fusion.6), channel_id=1, source_target_pairs={{0,1},{1,2},{2,3},{3,4},{4,5},{5,6},{6,7},{8,9},{9,10},{10,11},{11... | collective-permute-start | bytes 61448 | tf_op jit(solution)/shard_map/while/body/eval_jaxpr/ppermute | solution.py:29
  318.3 6.6 %collective-permute-start = (f32[5,4,256]{2,1,0:T(4,128)S(1)}, f32[5,4,256]{2,1,0:T(4,128)S(1)}, u32[]{:S(2)}, u32[]{:S(2)}) collective-permute-start(f32[5,4,256]{2,1,0:T(4,128)S(1)} %bitcast_add_fusion.6), channel_id=1, source_target_pairs={{0,1},{1,2},{2,3},{3,4},{4,5},{5,6},{6,7},{8,9},{9,10},{10,11},{11... | collective-permute-start | bytes 61448 | tf_op jit(solution)/shard_map/while/body/eval_jaxpr/ppermute | solution.py:29
  324.9 6.6 %collective-permute-start = (f32[5,4,256]{2,1,0:T(4,128)S(1)}, f32[5,4,256]{2,1,0:T(4,128)S(1)}, u32[]{:S(2)}, u32[]{:S(2)}) collective-permute-start(f32[5,4,256]{2,1,0:T(4,128)S(1)} %bitcast_add_fusion.6), channel_id=1, source_target_pairs={{0,1},{1,2},{2,3},{3,4},{4,5},{5,6},{6,7},{8,9},{9,10},{10,11},{11... | collective-permute-start | bytes 61448 | tf_op jit(solution)/shard_map/while/body/eval_jaxpr/ppermute | solution.py:29
  331.6 6.6 %collective-permute-start = (f32[5,4,256]{2,1,0:T(4,128)S(1)}, f32[5,4,256]{2,1,0:T(4,128)S(1)}, u32[]{:S(2)}, u32[]{:S(2)}) collective-permute-start(f32[5,4,256]{2,1,0:T(4,128)S(1)} %bitcast_add_fusion.6), channel_id=1, source_target_pairs={{0,1},{1,2},{2,3},{3,4},{4,5},{5,6},{6,7},{8,9},{9,10},{10,11},{11... | collective-permute-start | bytes 61448 | tf_op jit(solution)/shard_map/while/body/eval_jaxpr/ppermute | solution.py:29
  475.1 6.9 %collective-permute-start.1 = (f32[5,4,256]{2,1,0:T(4,128)S(1)}, f32[5,4,256]{2,1,0:T(4,128)S(1)}, u32[]{:S(2)}, u32[]{:S(2)}) collective-permute-start(f32[5,4,256]{2,1,0:T(4,128)S(1)} %bitcast_add_fusion.7), channel_id=1, source_target_pairs={{1,0},{2,1},{3,2},{4,3},{5,4},{6,5},{7,6},{9,8},{10,9},{11,10},{12... | collective-permute-start | bytes 61448 | tf_op jit(solution)/shard_map/while/body/eval_jaxpr/ppermute | solution.py:29
  482.0 6.9 %collective-permute-start.1 = (f32[5,4,256]{2,1,0:T(4,128)S(1)}, f32[5,4,256]{2,1,0:T(4,128)S(1)}, u32[]{:S(2)}, u32[]{:S(2)}) collective-permute-start(f32[5,4,256]{2,1,0:T(4,128)S(1)} %bitcast_add_fusion.7), channel_id=1, source_target_pairs={{1,0},{2,1},{3,2},{4,3},{5,4},{6,5},{7,6},{9,8},{10,9},{11,10},{12... | collective-permute-start | bytes 61448 | tf_op jit(solution)/shard_map/while/body/eval_jaxpr/ppermute | solution.py:29
  488.9 6.7 %collective-permute-start.1 = (f32[5,4,256]{2,1,0:T(4,128)S(1)}, f32[5,4,256]{2,1,0:T(4,128)S(1)}, u32[]{:S(2)}, u32[]{:S(2)}) collective-permute-start(f32[5,4,256]{2,1,0:T(4,128)S(1)} %bitcast_add_fusion.7), channel_id=1, source_target_pairs={{1,0},{2,1},{3,2},{4,3},{5,4},{6,5},{7,6},{9,8},{10,9},{11,10},{12... | collective-permute-start | bytes 61448 | tf_op jit(solution)/shard_map/while/body/eval_jaxpr/ppermute | solution.py:29
  495.6 6.5 %collective-permute-start.1 = (f32[5,4,256]{2,1,0:T(4,128)S(1)}, f32[5,4,256]{2,1,0:T(4,128)S(1)}, u32[]{:S(2)}, u32[]{:S(2)}) collective-permute-start(f32[5,4,256]{2,1,0:T(4,128)S(1)} %bitcast_add_fusion.7), channel_id=1, source_target_pairs={{1,0},{2,1},{3,2},{4,3},{5,4},{6,5},{7,6},{9,8},{10,9},{11,10},{12... | collective-permute-start | bytes 61448 | tf_op jit(solution)/shard_map/while/body/eval_jaxpr/ppermute | solution.py:29
  502.1 6.6 %collective-permute-start.1 = (f32[5,4,256]{2,1,0:T(4,128)S(1)}, f32[5,4,256]{2,1,0:T(4,128)S(1)}, u32[]{:S(2)}, u32[]{:S(2)}) collective-permute-start(f32[5,4,256]{2,1,0:T(4,128)S(1)} %bitcast_add_fusion.7), channel_id=1, source_target_pairs={{1,0},{2,1},{3,2},{4,3},{5,4},{6,5},{7,6},{9,8},{10,9},{11,10},{12... | collective-permute-start | bytes 61448 | tf_op jit(solution)/shard_map/while/body/eval_jaxpr/ppermute | solution.py:29
  508.8 6.6 %collective-permute-start.1 = (f32[5,4,256]{2,1,0:T(4,128)S(1)}, f32[5,4,256]{2,1,0:T(4,128)S(1)}, u32[]{:S(2)}, u32[]{:S(2)}) collective-permute-start(f32[5,4,256]{2,1,0:T(4,128)S(1)} %bitcast_add_fusion.7), channel_id=1, source_target_pairs={{1,0},{2,1},{3,2},{4,3},{5,4},{6,5},{7,6},{9,8},{10,9},{11,10},{12... | collective-permute-start | bytes 61448 | tf_op jit(solution)/shard_map/while/body/eval_jaxpr/ppermute | solution.py:29
  515.4 6.6 %collective-permute-start.1 = (f32[5,4,256]{2,1,0:T(4,128)S(1)}, f32[5,4,256]{2,1,0:T(4,128)S(1)}, u32[]{:S(2)}, u32[]{:S(2)}) collective-permute-start(f32[5,4,256]{2,1,0:T(4,128)S(1)} %bitcast_add_fusion.7), channel_id=1, source_target_pairs={{1,0},{2,1},{3,2},{4,3},{5,4},{6,5},{7,6},{9,8},{10,9},{11,10},{12... | collective-permute-start | bytes 61448 | tf_op jit(solution)/shard_map/while/body/eval_jaxpr/ppermute | solution.py:29
  (29 other events, 149.7 us)
Sparse Core Ops, SparseCore 0:
  10.6 22.4 reduce-scatter.3
  35.5 19.7 reduce-scatter.5
  81.8 20.4 reduce-scatter.7
where the time goes:
time: 544 us; the launch traced here: 542 us
  matrix products  246 us (45%)
  local copies, waits for them, and re-layouts  137 us (25%)
  waiting for transfers between devices  92 us (17%)
  starting transfers between devices  44 us (8%)
  between operations  13.3 us (2%)
  other arithmetic  7.49 us (1%)
    dot_general x16, matrix products, compose(): maps = jnp.einsum('ijap,jkap->ikap', factor, maps, precision=highest)  134 us
    dot_general x8, matrix products, apply_block(): return jnp.einsum('ijap,jap->iap', block, vector, precision=highest)  71.3 us
    ppermute x14, waiting for transfers between devices, passed_along(): lax.ppermute(value, axis, [(source, source + steps) for source in range(i...  47.7 us
    while x96, local copies, waits for them, and re-layouts  45.3 us
    neg x16, local copies, waits for them, and re-layouts, compose(): factor = -jnp.einsum('ijap,jk->ikap', block, matrix, precision=highest)  42.6 us
    ppermute x14, starting transfers between devices, passed_along(): lax.ppermute(value, axis, [(source, source + steps) for source in range(i...  41.3 us
    dynamic_slice x16, local copies, waits for them, and re-layouts, advance(): lax.dynamic_index_in_dim(inverse_diagonal, row_index, 3, keepdims=False)  19.6 us
    reduce_scatter x1, waiting for transfers between devices, body(): lax.psum_scatter(imag_part, 'pitch', scatter_dimension=3, tiled=True)  18.2 us
  transfers between devices with their start and end apart: 19, of which 17 were waited for; matrix products, arithmetic and copies ran while one was open for 8% of the time, Pallas kernels for 0%

commit v1 on v0

v1 whole, which is shorter than its diff:
```python
import jax
import jax.numpy as jnp
import numpy as np
from jax import lax
from jax.experimental import pallas as pl
from jax.experimental.pallas import tpu as pltpu
from jax.sharding import PartitionSpec as P

highest = lax.Precision.HIGHEST
LANES = 128
VMEM = pltpu.VMEM
SMEM = pltpu.SMEM


def exchange(blocks, axis, gather, collective):
    n = lax.axis_size(axis)
    part = blocks.shape if gather else blocks.shape[1:]

    def kernel(x_ref, o_ref, send, recv, own):
        me = lax.axis_index(axis)
        barrier = pltpu.get_barrier_semaphore()
        for step in range(1, n):
            pl.semaphore_signal(
                barrier,
                inc=1,
                device_id={axis: lax.rem(me + step, n)},
                device_id_type=pl.DeviceIdType.MESH,
            )
        local = pltpu.make_async_copy(x_ref if gather else x_ref.at[me], o_ref.at[me], own)
        local.start()
        pl.semaphore_wait(barrier, n - 1)
        copies = []
        for step in range(1, n):
            to = lax.rem(me + step, n)
            copy = pltpu.make_async_remote_copy(
                src_ref=x_ref if gather else x_ref.at[to],
                dst_ref=o_ref.at[me],
                send_sem=send.at[step - 1],
                recv_sem=recv.at[step - 1],
                device_id={axis: to},
                device_id_type=pl.DeviceIdType.MESH,
            )
            copy.start()
            copies.append(copy)
        local.wait()
        for copy in copies:
            copy.wait()

    return pl.pallas_call(
        kernel,
        out_shape=jax.ShapeDtypeStruct((n,) + part, jnp.float32),
        in_specs=[pl.BlockSpec(memory_space=VMEM)],
        out_specs=pl.BlockSpec(memory_space=VMEM),
        scratch_shapes=[
            pltpu.SemaphoreType.DMA((n - 1,)),
            pltpu.SemaphoreType.DMA((n - 1,)),
            pltpu.SemaphoreType.DMA,
        ],
        compiler_params=pltpu.CompilerParams(collective_id=collective, has_side_effects=True),
        name="exchange_%d" % collective,
    )(blocks)


def total(terms):
    result = terms[0]
    for term in terms[1:]:
        result = result + term
    return result


def scaled(block, matrix, nv):
    return [
        [-total([block[i][j] * matrix(j, k) for j in range(nv)]) for k in range(nv)]
        for i in range(nv)
    ]


def times(block, vector, nv):
    return [total([block[i][j] * vector[j] for j in range(nv)]) for i in range(nv)]


def load_block(diag, row, nv):
    return [[diag[i * nv + j, row] for j in range(nv)] for i in range(nv)]


def local_kernel(nv, coupling, diag, residual, neighbours, source, packed, maps, stars):
    rows = diag.shape[1]
    tile = diag.shape[2:]
    zero = jnp.zeros(tile, jnp.float32)
    one = jnp.ones(tile, jnp.float32)

    def entry(which):
        return lambda i, j: coupling[(which * nv + i) * nv + j]

    identity = [zero + (one if i == j else zero) for j in range(nv) for i in range(nv)]

    def column(flat, j):
        return flat[j * nv:(j + 1) * nv]

    def forward(row, carry):
        star, grown = list(carry[:nv]), list(carry[nv:])
        block = load_block(diag, row, nv)
        rhs = []
        for i in range(nv):
            value = residual[i, row]
            for side in range(4):
                matrix = entry(2 + side)
                for j in range(nv):
                    value = value - matrix(i, j) * neighbours[side * nv + j, row]
            source[i, row] = value
            rhs.append(value)
        step = scaled(block, entry(0), nv)
        star = [x + y for x, y in zip(times(block, rhs, nv), times(step, star, nv))]
        new = []
        for j in range(nv):
            new += times(step, column(grown, j), nv)
        for i in range(nv):
            stars[row, i] = star[i]
        for m in range(nv * nv):
            maps[row, m] = new[m]
        return tuple(star + new)

    last = lax.fori_loop(0, rows, forward, tuple([zero] * nv + identity))
    for m in range(nv + nv * nv):
        packed[m] = last[m]

    def backward(index, carry):
        row = rows - 1 - index
        nn = nv * nv
        base, response, grown = list(carry[:nv]), list(carry[nv:nv + nn]), list(carry[nv + nn:])
        step = scaled(load_block(diag, row, nv), entry(1), nv)
        base = [stars[row, i] + y for i, y in enumerate(times(step, base, nv))]
        new_response, new = [], []
        for j in range(nv):
            moved = times(step, column(response, j), nv)
            new_response += [maps[row, j * nv + i] + moved[i] for i in range(nv)]
            new += times(step, column(grown, j), nv)
        return tuple(base + new_response + new)

    initial = tuple([zero] * (nv + nv * nv) + identity)
    final = lax.fori_loop(0, rows, backward, initial)
    for m in range(nv + 2 * nv * nv):
        packed[nv + nv * nv + m] = final[m]


def solve_kernel(nv, got, out):
    n = got.shape[0]
    lanes = got.shape[2]
    nn = nv * nv

    def mapped(d, start, vector):
        return total(
            [
                got[d, start + j * nv:start + (j + 1) * nv, :] * vector[j:j + 1]
                for j in range(nv)
            ]
        )

    incoming = jnp.zeros((nv, lanes), jnp.float32)
    all_incoming = []
    for d in range(n):
        all_incoming.append(incoming)
        out[d, 0:nv, :] = incoming
        if d + 1 < n:
            incoming = got[d, 0:nv, :] + mapped(d, nv, incoming)
    following = jnp.zeros((nv, lanes), jnp.float32)
    base = nv + nn
    for d in reversed(range(n)):
        out[d, nv:2 * nv, :] = following
        if d > 0:
            known = got[d, base:base + nv, :] + mapped(d, base + nv, all_incoming[d])
            following = known + mapped(d, base + nv + nn, following)


def final_kernel(nv, coupling, diag, source, incoming, update, stars):
    rows = diag.shape[1]

    def mixed(which, vector):
        return [
            total([coupling[(which * nv + i) * nv + j] * vector[j] for j in range(nv)])
            for i in range(nv)
        ]

    def forward(row, star):
        pushed = mixed(0, star)
        rhs = [source[i, row] - pushed[i] for i in range(nv)]
        star = times(load_block(diag, row, nv), rhs, nv)
        for i in range(nv):
            stars[row, i] = star[i]
        return tuple(star)

    lax.fori_loop(0, rows, forward, tuple(incoming[i] for i in range(nv)))

    def backward(index, following):
        row = rows - 1 - index
        moved = times(load_block(diag, row, nv), mixed(1, following), nv)
        value = [stars[row, i] - moved[i] for i in range(nv)]
        for i in range(nv):
            update[i, row] = value[i]
        return tuple(value)

    lax.fori_loop(0, rows, backward, tuple(incoming[nv + i] for i in range(nv)))


def tables(n, width, harmonics):
    points = n * width
    own = harmonics // n
    k = n * np.arange(own)[None, :] + np.arange(n)[:, None]
    product = (np.arange(width)[None, :, None] * k[:, None, :]) % points
    angle = product * (2.0 * np.pi / points)
    return np.stack([np.cos(angle), np.sin(angle)], axis=1).astype(np.float32)


def corrections(residual, prior, characteristic, cutoffs):
    n = lax.axis_size("pitch")
    me = lax.axis_index("pitch")
    nv, _, rows, width = residual.shape
    harmonics = characteristic.shape[2]
    points = n * width
    own = harmonics // n
    flat_rows = 2 * nv * rows
    planes = jnp.stack([residual[:, 0], residual[:, -1]]).reshape(flat_rows, width)
    edges = jnp.stack([prior[..., 0], prior[..., -1]]).reshape(-1)
    edge_rows = -(-edges.shape[0] // width)
    edge_rows = -(-edge_rows // 8) * 8
    edges = jnp.pad(edges, (0, edge_rows * width - edges.shape[0])).reshape(edge_rows, width)
    gathered = exchange(jnp.concatenate([planes, edges]), "pitch", True, 0)

    edge_shape = (2,) + prior.shape[:-1]
    count = int(np.prod(edge_shape))

    def edges_of(device):
        piece = lax.dynamic_index_in_dim(gathered, device, 0, keepdims=False)[flat_rows:]
        return piece.reshape(-1)[:count].reshape(edge_shape)

    before = edges_of(lax.rem(me + n - 1, n))[1][..., None]
    after = edges_of(lax.rem(me + 1, n))[0][..., None]

    turn = 2.0 * np.pi * (np.arange(n)[:, None] * np.arange(n)[None, :] % n) / n
    turn_cos = lax.dynamic_index_in_dim(jnp.asarray(np.cos(turn), jnp.float32), me, 0, keepdims=False)
    turn_sin = lax.dynamic_index_in_dim(jnp.asarray(np.sin(turn), jnp.float32), me, 0, keepdims=False)
    waves = total([gathered[q, :flat_rows] * turn_cos[q] for q in range(n)])
    waves_imag = -total([gathered[q, :flat_rows] * turn_sin[q] for q in range(n)])
    table = lax.dynamic_index_in_dim(jnp.asarray(tables(n, width, harmonics)), me, 0, keepdims=False)
    cosine, sine = table[0], table[1]
    both = jnp.concatenate([waves, waves_imag], axis=1)
    matrix = jnp.concatenate(
        [jnp.concatenate([cosine, -sine], axis=1), jnp.concatenate([sine, cosine], axis=1)]
    )
    spectrum = jnp.dot(both, matrix, precision=highest).reshape(2, nv, rows, 2 * own)
    real_part, imag_part = spectrum[..., :own], spectrum[..., own:]

    mine = n * jnp.arange(own, dtype=jnp.int32) + me
    chosen = (jnp.arange(harmonics, dtype=jnp.int32)[:, None] == mine[None, :]).astype(jnp.float32)
    by_entry = characteristic.transpose(3, 4, 0, 1, 2).reshape(-1, harmonics)
    picked = jnp.dot(by_entry, chosen, precision=highest).reshape(nv, nv, 2, 2, 1, own)
    out_real, out_imag = [], []
    kept = (mine[None, :] < cutoffs[:, None]).astype(jnp.float32)
    weight = jnp.where(mine == 0, 1.0, 2.0).astype(jnp.float32) / points
    factor = (kept * weight[None, :])[:, None, :]
    for i in range(nv):
        cr = [picked[i, j, :, 0] for j in range(nv)]
        ci = [picked[i, j, :, 1] for j in range(nv)]
        out_real.append(
            total([cr[j] * real_part[:, j] - ci[j] * imag_part[:, j] for j in range(nv)]) * factor
        )
        out_imag.append(
            total([cr[j] * imag_part[:, j] + ci[j] * real_part[:, j] for j in range(nv)]) * factor
        )
    corrected = jnp.concatenate(
        [jnp.stack(out_real, axis=1), jnp.stack(out_imag, axis=1)], axis=-1
    ).reshape(flat_rows, 2 * own)
    back = jnp.concatenate(
        [
            jnp.concatenate([cosine.T, sine.T], axis=1),
            jnp.concatenate([-sine.T, cosine.T], axis=1),
        ]
    )
    field = jnp.dot(corrected, back, precision=highest)
    parts = jnp.stack(
        [field[:, :width] * turn_cos[q] - field[:, width:] * turn_sin[q] for q in range(n)]
    )
    received = exchange(parts, "pitch", False, 1)
    correction = received.sum(axis=0).reshape(2, nv, rows, width)
    return correction, before, after


def body(residual, inverse_diagonal, prior, coupling, characteristic, cutoffs):
    nv, axial, rows, width = residual.shape
    cells = axial * width
    tile = (cells // LANES, LANES)
    n = lax.axis_size("span")

    def by_row(field):
        lead = field.shape[:-3]
        return jnp.moveaxis(field, -2, -3).reshape((-1, rows) + tile)

    diag = by_row(inverse_diagonal)
    correction, before, after = corrections(residual, prior, characteristic, cutoffs)
    corrected = by_row(residual.at[:, 0].add(correction[0]).at[:, -1].add(correction[1]))
    blank = jnp.zeros_like(prior[:, :1])
    neighbours = by_row(
        jnp.stack(
            [
                jnp.concatenate([before, prior[..., :-1]], axis=3),
                jnp.concatenate([prior[..., 1:], after], axis=3),
                jnp.concatenate([blank, prior[:, :-1]], axis=1),
                jnp.concatenate([prior[:, 1:], blank], axis=1),
            ]
        )
    )
    scalars = coupling.reshape(-1)
    nn = nv * nv
    count = 2 * nv + 3 * nn
    smem = pl.BlockSpec(memory_space=SMEM)
    vmem = pl.BlockSpec(memory_space=VMEM)
    source, packed = pl.pallas_call(
        lambda *refs: local_kernel(nv, *refs),
        out_shape=(
            jax.ShapeDtypeStruct((nv, rows) + tile, jnp.float32),
            jax.ShapeDtypeStruct((count,) + tile, jnp.float32),
        ),
        in_specs=[smem, vmem, vmem, vmem],
        out_specs=(vmem, vmem),
        scratch_shapes=[
            VMEM((rows, nn) + tile, jnp.float32),
            VMEM((rows, nv) + tile, jnp.float32),
        ],
        name="local_sweeps",
    )(scalars, diag, corrected, neighbours)
    share = cells // n
    blocks = packed.reshape(count, n, share).transpose(1, 0, 2)
    got = exchange(blocks, "span", False, 2)
    solved = pl.pallas_call(
        lambda *refs: solve_kernel(nv, *refs),
        out_shape=jax.ShapeDtypeStruct((n, 2 * nv, share), jnp.float32),
        in_specs=[vmem],
        out_specs=vmem,
        name="solve",
    )(got)
    back = exchange(solved, "span", False, 3)
    incoming = back.transpose(1, 0, 2).reshape((2 * nv,) + tile)
    update = pl.pallas_call(
        lambda *refs: final_kernel(nv, *refs),
        out_shape=jax.ShapeDtypeStruct((nv, rows) + tile, jnp.float32),
        in_specs=[smem, vmem, vmem, vmem],
        out_specs=vmem,
        scratch_shapes=[VMEM((rows, nv) + tile, jnp.float32)],
        name="final_sweeps",
    )(scalars, diag, source, incoming)
    return jnp.moveaxis(update.reshape(nv, rows, axial, width), 1, 2)


def solution(mesh):
    in_specs = (
        P(None, None, "span", "pitch"),
        P(None, None, None, "span", "pitch"),
        P(None, None, "span", "pitch"),
        P(),
        P(),
        P(),
    )
    out_specs = P(None, None, "span", "pitch")
    return jax.shard_map(body, mesh=mesh, in_specs=in_specs, out_specs=out_specs, check_vma=False)
```

time: 544 us -> 81.8 us (0.15)
  matrix products: 246 us -> 1.29 us
  local copies, waits for them, and re-layouts: 137 us -> 17.4 us
  waiting for transfers between devices: 92 us -> 0 us
  Pallas kernels: 0 us -> 48.1 us
  starting transfers between devices: 44 us -> 0 us
  between operations: 13.3 us -> 0.37 us
  other arithmetic: 7.49 us -> 13.8 us
    dot_general x68 -> x3, matrix products: 246 us -> 1.29 us  [the longest x1 0.62 us: corrections(): field = jnp.dot(corrected, back, precision=highest)]
    while x100 -> x0, local copies, waits for them, and re-layouts: 50.7 us -> none
    pallas_call x0 -> x7, Pallas kernels: none -> 48.1 us  [the longest x4 39.8 us: exchange(): pl.pallas_call(kernel, out_shape=jax.ShapeDtypeStruct((n,) + part, jnp.fl...]
    ppermute x16 -> x0, waiting for transfers between devices: 47.7 us -> none  [the longest x14 47.7 us: passed_along(): lax.ppermute(value, axis, [(source, source + steps) for source in range(i...]
    reduce_scatter x3 -> x0, waiting for transfers between devices: 44.3 us -> none  [the longest x1 18.2 us: body(): lax.psum_scatter(imag_part, 'pitch', scatter_dimension=3, tiled=True)]
    ppermute x16 -> x0, starting transfers between devices: 43.7 us -> none  [the longest x14 41.3 us: passed_along(): lax.ppermute(value, axis, [(source, source + steps) for source in range(i...]
    neg x16 -> x0, local copies, waits for them, and re-layouts: 42.6 us -> none  [compose(): factor = -jnp.einsum('ijap,jk->ikap', block, matrix, precision=highest)]
    dynamic_slice x48 -> x1, local copies, waits for them, and re-layouts: 20.3 us -> 0.71 us  [corrections(): lax.dynamic_index_in_dim(jnp.asarray(np.sin(turn), jnp.float32), me, 0, k...]
  transfers between devices with their start and end apart: 19 -> 0, of which waited for: 17 -> 0; matrix products, arithmetic and copies ran while one was open for 8% -> 0% of each run, Pallas kernels for 0% -> 0%
where the time goes in v1:
time: 81.8 us; the launch traced here: 80.9 us
  Pallas kernels  48.1 us (59%)
  local copies, waits for them, and re-layouts  17.4 us (21%)
  other arithmetic  13.8 us (17%)
  matrix products  1.29 us (2%)
    pallas_call x4, Pallas kernels, exchange(): pl.pallas_call(kernel, out_shape=jax.ShapeDtypeStruct((n,) + part, jnp.fl...  39.8 us
    add x1, other arithmetic, total(): result = result + term  5.94 us
    another operation x2, other arithmetic, corrections(): jnp.stack([field[:, :width] * turn_cos[q] - field[:, width:] * turn_sin[q...  5.69 us
    pallas_call x1, Pallas kernels, body(): pl.pallas_call(lambda *refs: local_kernel(nv, *refs), out_shape=(jax.Shap...  4.2 us
    reshape x3, local copies, waits for them, and re-layouts, by_row(): return jnp.moveaxis(field, -2, -3).reshape((-1, rows) + tile)  3.1 us
    unnamed x13, local copies, waits for them, and re-layouts  2.64 us
    pallas_call x1, Pallas kernels, body(): pl.pallas_call(lambda *refs: final_kernel(nv, *refs), out_shape=jax.Shape...  2.34 us
    pallas_call x1, local copies, waits for them, and re-layouts, body(): pl.pallas_call(lambda *refs: local_kernel(nv, *refs), out_shape=(jax.Shap...  1.79 us

profile of v1, /device:TPU:0, one launch (start us, length us, event | category | flops | bytes accessed | tf_op | source)
XLA Modules:
  0.0 80.9 jit_solution(10288571973967305)
XLA Ops:
  0.0 0.9 %copy.51 = f32[5,4,8,256]{3,2,1,0:T(8,128)S(1)} copy(f32[5,4,8,256]{3,2,1,0:T(8,128)} %param.13) | data formatting | bytes 327680
  0.9 0.7 reshape.268.refs_0_
  1.6 1.5 %copy.21 = f32[5,5,8,4,256]{4,3,2,1,0:T(4,128)S(1)} copy(f32[5,5,8,4,256]{4,2,3,1,0:T(8,128)} %bitcast.147) | data formatting | bytes 1638400 | tf_op jit(solution)/shard_map/transpose | solution.py:296
  3.1 1.2 %reshape.269.refs_1_ = f32[25,8,8,128]{3,2,1,0:T(8,128)} reshape(f32[5,5,8,4,256]{4,3,2,1,0:T(4,128)S(1)} %copy.21) | data formatting | bytes 1638400 | tf_op jit(solution)/shard_map/reshape | solution.py:296
  5.7 0.9 %copy-done = f32[5,4,8,256]{3,2,1,0:T(8,128)S(1)} copy-done((f32[5,4,8,256]{3,2,1,0:T(8,128)S(1)}, f32[5,4,8,256]{3,2,1,0:T(8,128)}, u32[]{:S(2)}) %copy-start) | copy-done | bytes 163864
  7.7 9.0 %exchange_0.1 = f32[4,88,256]{2,1,0:T(8,128)} custom-call(f32[88,256]{1,0:T(8,128)} %pad_maximum_fusion.1.x_ref), custom_call_target="tpu_custom_call" | custom-call | tf_op jit(solution)/shard_map/exchange_0/pallas_call | solution.py:49
  16.8 0.7 constant_dynamic-slice_fusion.2
  18.7 5.9 %add_bitcast_fusion = (f32[80,256]{1,0:T(8,128)S(1)}, f32[80,256]{1,0:T(8,128)S(1)}) fusion(f32[4,88,256]{2,1,0:T(8,128)} %exchange_0.1, f32[]{:T(128)} %bitcast.11, f32[]{:T(128)} %bitcast.10, f32[]{:T(128)} %bitcast.9, f32[]{:T(128)} %bitcast.8, f32[]{:T(128)} %bitcast.16, f32[]{:T(128)} %bitcast.15, f32[]{:T(128)} %bitcast.14, f32[]{:T(128)} %bitcast.13), kind=kLoop, calls=%fused_computation.42 | loop fusion | flops 307200 | bytes 491552 | tf_op jit(solution)/shard_map/add | solution.py:67
  26.1 4.9 %subtract_bitcast_fusion.3 = (f32[1,80,256]{2,1,0:T(8,128)S(1)}, f32[1,80,256]{2,1,0:T(8,128)S(1)}, f32[1,80,256]{2,1,0:T(8,128)S(1)}, f32[1,80,256]{2,1,0:T(8,128)S(1)}) fusion(f32[80,512]{1,0:T(8,128)S(1)} %fusion.8, f32[]{:T(128)} %bitcast.13, f32[]{:T(128)} %bitcast.8, f32[]{:T(128)} %bitcast.15, f32[]{:T(128)} %bitcast.10, f32[]{:T(128)} %bitcast.16, ...), kind=kLoop, calls=%fused_computation.41 | loop fusion | flops 245760 | bytes 491552 | tf_op jit(solution)/shard_map/stack | solution.py:280
  31.0 0.8 pad_maximum_fusion.x_ref
  31.8 7.7 %exchange_1.1 = f32[4,80,256]{2,1,0:T(8,128)} custom-call(f32[4,80,256]{2,1,0:T(8,128)} %pad_maximum_fusion.x_ref), custom_call_target="tpu_custom_call" | custom-call | tf_op jit(solution)/shard_map/exchange_1/pallas_call | solution.py:49
  39.5 1.0 %reduce_sum.9 = f32[80,256]{1,0:T(8,128)S(1)} reduce(f32[4,80,256]{2,1,0:T(8,128)} %exchange_1.1, f32[]{:T(128)} %constant.100.clone.1), dimensions={0}, to_apply=%region_0.1 | reduce | flops 61440 | bytes 409604 | tf_op jit(solution)/shard_map/reduce_sum | solution.py:284
  40.6 0.7 reshape.279.refs_2_
  41.5 0.7 constant_dynamic-slice_fusion.1
  43.5 1.1 %reshape.280.refs_3_ = f32[20,8,8,128]{3,2,1,0:T(8,128)} reshape(f32[4,5,8,4,256]{4,3,2,1,0:T(4,128)S(1)} %copy.28) | data formatting | bytes 1310720 | tf_op jit(solution)/shard_map/reshape | solution.py:296
  44.6 4.2 %local_sweeps.1 = (f32[5,8,8,128]{3,2,1,0:T(8,128)}, f32[85,8,128]{2,1,0:T(8,128)}) custom-call(f32[150]{0:T(256)} %reshape.268.refs_0_, f32[25,8,8,128]{3,2,1,0:T(8,128)} %reshape.269.refs_1_, f32[5,8,8,128]{3,2,1,0:T(8,128)} %reshape.279.refs_2_, f32[20,8,8,128]{3,2,1,0:T(8,128)} %reshape.280.refs_3_), custom_call_target="tpu_custom_call" | custom-call | tf_op jit(solution)/shard_map/local_sweeps/pallas_call | solution.py:317
  48.8 1.8 %copy.37 = f32[85,8,128]{2,0,1:T(8,128)} copy(f32[85,8,128]{2,1,0:T(8,128)} %get-tuple-element.32) | data formatting | bytes 696320 | tf_op jit(solution)/shard_map/local_sweeps/pallas_call | solution.py:317
  50.6 13.1 %exchange_2.1.refs_0_ = f32[8,85,128]{2,1,0:T(8,128)} custom-call(f32[8,85,128]{2,1,0:T(8,128)} %bitcast.146), custom_call_target="tpu_custom_call" | custom-call | tf_op jit(solution)/shard_map/exchange_2/pallas_call | solution.py:49
  63.7 1.7 %solve.1.x_ref = f32[8,10,128]{2,1,0:T(8,128)} custom-call(f32[8,85,128]{2,1,0:T(8,128)} %exchange_2.1.refs_0_), custom_call_target="tpu_custom_call" | custom-call | tf_op jit(solution)/shard_map/solve/pallas_call | solution.py:334
  65.4 10.0 %exchange_3.1 = f32[8,10,128]{2,1,0:T(8,128)} custom-call(f32[8,10,128]{2,1,0:T(8,128)} %solve.1.x_ref), custom_call_target="tpu_custom_call" | custom-call | tf_op jit(solution)/shard_map/exchange_3/pallas_call | solution.py:49
  75.4 1.5 %copy.39 = f32[8,10,128]{2,0,1:T(8,128)} copy(f32[8,10,128]{2,1,0:T(8,128)} %exchange_3.1) | data formatting | bytes 81920 | tf_op jit(solution)/shard_map/exchange_3/pallas_call | solution.py:49
  76.9 2.3 %final_sweeps.1 = f32[5,8,8,128]{3,2,1,0:T(8,128)} custom-call(f32[150]{0:T(256)} %reshape.268.refs_0_, f32[25,8,8,128]{3,2,1,0:T(8,128)} %reshape.269.refs_1_, f32[5,8,8,128]{3,2,1,0:T(8,128)} %get-tuple-element.31.refs_2_, f32[10,8,128]{2,1,0:T(8,128)} %bitcast.150), custom_call_target="tpu_custom_call" | custom-call | tf_op jit(solution)/shard_map/final_sweeps/pallas_call | solution.py:343
  79.2 1.0 %reshape.281 = f32[5,8,4,256]{3,2,1,0:T(4,128)S(1)} reshape(f32[5,8,8,128]{3,2,1,0:T(8,128)} %final_sweeps.1) | data formatting | bytes 327680 | tf_op jit(solution)/shard_map/reshape | solution.py:351
  80.2 0.7 copy.38
  (62 shorter events, 6.4 us)
Async XLA Ops:
  0.0 0.9 %copy-start.3 = (f32[6,5,5]{2,0,1:T(8,128)S(1)}, f32[6,5,5]{2,0,1:T(8,128)}, u32[]{:S(2)}) copy-start(f32[6,5,5]{2,0,1:T(8,128)} %param.16) | copy-start | bytes 1804
  3.1 1.3 %copy-start.4 = (s32[2]{0:T(128)S(1)}, s32[2]{0:T(128)}, u32[]{:S(2)}) copy-start(s32[2]{0:T(128)} %param.18) | copy-start | bytes 28
  3.1 1.3 %copy-start.2 = (f32[2,2,512,5,5]{2,1,4,3,0:T(2,128)S(1)}, f32[2,2,512,5,5]{2,1,4,3,0:T(2,128)}, u32[]{:S(2)}) copy-start(f32[2,2,512,5,5]{2,1,4,3,0:T(2,128)} %param.17) | copy-start | bytes 614404
  4.4 1.2 %copy-start.1 = (f32[4,2,256,128]{3,2,1,0:T(8,128)S(1)}, f32[4,2,256,128]{3,2,1,0:T(8,128)}, u32[]{:S(2)}) copy-start(f32[4,2,256,128]{3,2,1,0:T(8,128)} %constant.109.clone) | copy-start | bytes 3145732
  5.6 0.9 %copy-start = (f32[5,4,8,256]{3,2,1,0:T(8,128)S(1)}, f32[5,4,8,256]{3,2,1,0:T(8,128)}, u32[]{:S(2)}) copy-start(f32[5,4,8,256]{3,2,1,0:T(8,128)} %param.15) | copy-start | bytes 491524

commit v2 on v1

--- a/solution.py
+++ b/solution.py
@@ -12,53 +12,50 @@
 SMEM = pltpu.SMEM
 
 
-def exchange(blocks, axis, gather, collective):
+def greet(axis):
     n = lax.axis_size(axis)
-    part = blocks.shape if gather else blocks.shape[1:]
-
-    def kernel(x_ref, o_ref, send, recv, own):
-        me = lax.axis_index(axis)
-        barrier = pltpu.get_barrier_semaphore()
-        for step in range(1, n):
-            pl.semaphore_signal(
-                barrier,
-                inc=1,
-                device_id={axis: lax.rem(me + step, n)},
-                device_id_type=pl.DeviceIdType.MESH,
-            )
-        local = pltpu.make_async_copy(x_ref if gather else x_ref.at[me], o_ref.at[me], own)
-        local.start()
-        pl.semaphore_wait(barrier, n - 1)
-        copies = []
-        for step in range(1, n):
-            to = lax.rem(me + step, n)
-            copy = pltpu.make_async_remote_copy(
-                src_ref=x_ref if gather else x_ref.at[to],
-                dst_ref=o_ref.at[me],
-                send_sem=send.at[step - 1],
-                recv_sem=recv.at[step - 1],
-                device_id={axis: to},
-                device_id_type=pl.DeviceIdType.MESH,
-            )
-            copy.start()
-            copies.append(copy)
-        local.wait()
-        for copy in copies:
-            copy.wait()
-
-    return pl.pallas_call(
-        kernel,
-        out_shape=jax.ShapeDtypeStruct((n,) + part, jnp.float32),
-        in_specs=[pl.BlockSpec(memory_space=VMEM)],
-        out_specs=pl.BlockSpec(memory_space=VMEM),
-        scratch_shapes=[
-            pltpu.SemaphoreType.DMA((n - 1,)),
-            pltpu.SemaphoreType.DMA((n - 1,)),
-            pltpu.SemaphoreType.DMA,
-        ],
-        compiler_params=pltpu.CompilerParams(collective_id=collective, has_side_effects=True),
-        name="exchange_%d" % collective,
-    )(blocks)
+    me = lax.axis_index(axis)
+    barrier = pltpu.get_barrier_semaphore()
+    for step in range(1, n):
+        pl.semaphore_signal(
+            barrier,
+            inc=1,
+            device_id={axis: lax.rem(me + step, n)},
+            device_id_type=pl.DeviceIdType.MESH,
+        )
+
+
+def greeted(axis):
+    pl.semaphore_wait(pltpu.get_barrier_semaphore(), lax.axis_size(axis) - 1)
+
+
+def start_exchange(source, target, send, recv, axis, gather):
+    n = lax.axis_size(axis)
+    me = lax.axis_index(axis)
+    copies = []
+    for step in range(1, n):
+        to = lax.rem(me + step, n)
+        copy = pltpu.make_async_remote_copy(
+            src_ref=source if gather else source.at[to],
+            dst_ref=target.at[me],
+            send_sem=send.at[step - 1],
+            recv_sem=recv.at[step - 1],
+            device_id={axis: to},
+            device_id_type=pl.DeviceIdType.MESH,
+        )
+        copy.start()
+        copies.append(copy)
+    return copies
+
+
+def wait_all(copies):
+    for copy in copies:
+        copy.wait()
+
+
+def semaphores(axis, exchanges):
+    n = lax.axis_size(axis)
+    return [pltpu.SemaphoreType.DMA((n - 1,)) for _ in range(2 * exchanges)]
 
 
 def total(terms):
@@ -202,6 +199,96 @@
     lax.fori_loop(0, rows, backward, tuple(incoming[nv + i] for i in range(nv)))
 
 
+def spectral_kernel(
+    nv, rows, turn, x_ref, table, picked, factor, out, edges, got, parts, landed, s0, r0, s1, r1
+):
+    n = lax.axis_size("pitch")
+    me = lax.axis_index("pitch")
+    flat = 2 * nv * rows
+    greet("pitch")
+    got[me] = x_ref[...]
+    greeted("pitch")
+    wait_all(start_exchange(x_ref, got, s0, r0, "pitch", True))
+    edges[...] = got[:, flat:, :]
+    waves = total([got[q, :flat, :] * turn[q] for q in range(n)])
+    waves_imag = -total([got[q, :flat, :] * turn[n + q] for q in range(n)])
+    both = jnp.concatenate([waves, waves_imag])
+    cosine, sine = table[0], table[1]
+    with_cos = jnp.dot(both, cosine, precision=highest, preferred_element_type=jnp.float32)
+    with_sin = jnp.dot(both, sine, precision=highest, preferred_element_type=jnp.float32)
+    real_part = with_cos[:flat] + with_sin[flat:]
+    imag_part = with_cos[flat:] - with_sin[:flat]
+    out_real, out_imag = [], []
+    for q in range(2):
+        weight = factor[q:q + 1, :]
+        sr = [real_part[(q * nv + j) * rows:(q * nv + j + 1) * rows] for j in range(nv)]
+        si = [imag_part[(q * nv + j) * rows:(q * nv + j + 1) * rows] for j in range(nv)]
+        for i in range(nv):
+            at = [((i * nv + j) * 2 + q) * 2 for j in range(nv)]
+            cr = [picked[m:m + 1, :] for m in at]
+            ci = [picked[m + 1:m + 2, :] for m in at]
+            out_real.append(total([cr[j] * sr[j] - ci[j] * si[j] for j in range(nv)]) * weight)
+            out_imag.append(total([cr[j] * si[j] + ci[j] * sr[j] for j in range(nv)]) * weight)
+    stacked = jnp.concatenate(out_real + out_imag)
+
+    def back(matrix):
+        return lax.dot_general(
+            stacked,
+            matrix,
+            (((1,), (1,)), ((), ())),
+            precision=highest,
+            preferred_element_type=jnp.float32,
+        )
+
+    with_cos, with_sin = back(cosine), back(sine)
+    field = with_cos[:flat] - with_sin[flat:]
+    field_imag = with_sin[:flat] + with_cos[flat:]
+    for q in range(n):
+        parts[q] = field * turn[q] - field_imag * turn[n + q]
+    copies = start_exchange(parts, landed, s1, r1, "pitch", False)
+    landed[me] = parts[me]
+    wait_all(copies)
+    out[...] = total([landed[q] for q in range(n)])
+
+
+def sweeps_kernel(
+    nv, coupling, diag, residual, neighbours, update,
+    source, maps, stars, packed, send, got, solved, back, incoming, s0, r0, s1, r1
+):
+    n = lax.axis_size("span")
+    me = lax.axis_index("span")
+    share = send.shape[2]
+    pieces = LANES // share
+    greet("span")
+    local_kernel(nv, coupling, diag, residual, neighbours, source, packed, maps, stars)
+    for m in range(packed.shape[0]):
+        value = packed[m]
+        if pieces == 1:
+            send[:, m, :] = value
+        else:
+            for d in range(n):
+                lane = d % pieces * share
+                row = d // pieces
+                send[d, m:m + 1, :] = value[row:row + 1, lane:lane + share]
+    greeted("span")
+    copies = start_exchange(send, got, s0, r0, "span", False)
+    got[me] = send[me]
+    wait_all(copies)
+    solve_kernel(nv, got, solved)
+    copies = start_exchange(solved, back, s1, r1, "span", False)
+    back[me] = solved[me]
+    wait_all(copies)
+    for m in range(2 * nv):
+        if pieces == 1:
+            incoming[m] = back[:, m, :]
+        else:
+            for d in range(n):
+                lane = d % pieces * share
+                row = d // pieces
+                incoming[m, row:row + 1, lane:lane + share] = back[d, m:m + 1, :]
+    final_kernel(nv, coupling, diag, source, incoming, update, stars)
+
+
 def tables(n, width, harmonics):
     points = n * width
     own = harmonics // n
@@ -224,65 +311,54 @@
     edge_rows = -(-edges.shape[0] // width)
     edge_rows = -(-edge_rows // 8) * 8
     edges = jnp.pad(edges, (0, edge_rows * width - edges.shape[0])).reshape(edge_rows, width)
-    gathered = exchange(jnp.concatenate([planes, edges]), "pitch", True, 0)
-
-    edge_shape = (2,) + prior.shape[:-1]
-    count = int(np.prod(edge_shape))
-
-    def edges_of(device):
-        piece = lax.dynamic_index_in_dim(gathered, device, 0, keepdims=False)[flat_rows:]
-        return piece.reshape(-1)[:count].reshape(edge_shape)
-
-    before = edges_of(lax.rem(me + n - 1, n))[1][..., None]
-    after = edges_of(lax.rem(me + 1, n))[0][..., None]
-
     turn = 2.0 * np.pi * (np.arange(n)[:, None] * np.arange(n)[None, :] % n) / n
     turn_cos = lax.dynamic_index_in_dim(jnp.asarray(np.cos(turn), jnp.float32), me, 0, keepdims=False)
     turn_sin = lax.dynamic_index_in_dim(jnp.asarray(np.sin(turn), jnp.float32), me, 0, keepdims=False)
-    waves = total([gathered[q, :flat_rows] * turn_cos[q] for q in range(n)])
-    waves_imag = -total([gathered[q, :flat_rows] * turn_sin[q] for q in range(n)])
     table = lax.dynamic_index_in_dim(jnp.asarray(tables(n, width, harmonics)), me, 0, keepdims=False)
-    cosine, sine = table[0], table[1]
-    both = jnp.concatenate([waves, waves_imag], axis=1)
-    matrix = jnp.concatenate(
-        [jnp.concatenate([cosine, -sine], axis=1), jnp.concatenate([sine, cosine], axis=1)]
-    )
-    spectrum = jnp.dot(both, matrix, precision=highest).reshape(2, nv, rows, 2 * own)
-    real_part, imag_part = spectrum[..., :own], spectrum[..., own:]
-
     mine = n * jnp.arange(own, dtype=jnp.int32) + me
     chosen = (jnp.arange(harmonics, dtype=jnp.int32)[:, None] == mine[None, :]).astype(jnp.float32)
     by_entry = characteristic.transpose(3, 4, 0, 1, 2).reshape(-1, harmonics)
-    picked = jnp.dot(by_entry, chosen, precision=highest).reshape(nv, nv, 2, 2, 1, own)
-    out_real, out_imag = [], []
+    picked = jnp.dot(by_entry, chosen, precision=highest)
     kept = (mine[None, :] < cutoffs[:, None]).astype(jnp.float32)
     weight = jnp.where(mine == 0, 1.0, 2.0).astype(jnp.float32) / points
-    factor = (kept * weight[None, :])[:, None, :]
-    for i in range(nv):
-        cr = [picked[i, j, :, 0] for j in range(nv)]
-        ci = [picked[i, j, :, 1] for j in range(nv)]
-        out_real.append(
-            total([cr[j] * real_part[:, j] - ci[j] * imag_part[:, j] for j in range(nv)]) * factor
-        )
-        out_imag.append(
-            total([cr[j] * imag_part[:, j] + ci[j] * real_part[:, j] for j in range(nv)]) * factor
-        )
-    corrected = jnp.concatenate(
-        [jnp.stack(out_real, axis=1), jnp.stack(out_imag, axis=1)], axis=-1
-    ).reshape(flat_rows, 2 * own)
-    back = jnp.concatenate(
-        [
-            jnp.concatenate([cosine.T, sine.T], axis=1),
-            jnp.concatenate([-sine.T, cosine.T], axis=1),
+    factor = kept * weight[None, :]
+    smem = pl.BlockSpec(memory_space=SMEM)
+    vmem = pl.BlockSpec(memory_space=VMEM)
+    total_rows = flat_rows + edge_rows
+    correction, gathered = pl.pallas_call(
+        lambda *refs: spectral_kernel(nv, rows, *refs),
+        out_shape=(
+            jax.ShapeDtypeStruct((flat_rows, width), jnp.float32),
+            jax.ShapeDtypeStruct((n, edge_rows, width), jnp.float32),
+        ),
+        in_specs=[smem, vmem, vmem, vmem, vmem],
+        out_specs=(vmem, vmem),
+        scratch_shapes=[
+            VMEM((n, total_rows, width), jnp.float32),
+            VMEM((n, flat_rows, width), jnp.float32),
+            VMEM((n, flat_rows, width), jnp.float32),
         ]
+        + semaphores("pitch", 2),
+        compiler_params=pltpu.CompilerParams(collective_id=0, has_side_effects=True),
+        name="spectral",
+    )(
+        jnp.concatenate([turn_cos, turn_sin]),
+        jnp.concatenate([planes, edges]),
+        table,
+        picked,
+        factor,
     )
-    field = jnp.dot(corrected, back, precision=highest)
-    parts = jnp.stack(
-        [field[:, :width] * turn_cos[q] - field[:, width:] * turn_sin[q] for q in range(n)]
-    )
-    received = exchange(parts, "pitch", False, 1)
-    correction = received.sum(axis=0).reshape(2, nv, rows, width)
-    return correction, before, after
+    edge_shape = (2,) + prior.shape[:-1]
+    count = int(np.prod(edge_shape))
+
+    def edges_of(device):
+        piece = lax.dynamic_index_in_dim(gathered, device, 0, keepdims=False)
+        return piece.reshape(-1)[:count].reshape(edge_shape)
+
+    before = edges_of(lax.rem(me + n - 1, n))[1][..., None]
+    after = edges_of(lax.rem(me + 1, n))[0][..., None]
+
+    return correction.reshape(2, nv, rows, width), before, after
 
 
 def body(residual, inverse_diagonal, prior, coupling, characteristic, cutoffs):
@@ -314,40 +390,27 @@
     count = 2 * nv + 3 * nn
     smem = pl.BlockSpec(memory_space=SMEM)
     vmem = pl.BlockSpec(memory_space=VMEM)
-    source, packed = pl.pallas_call(
-        lambda *refs: local_kernel(nv, *refs),
-        out_shape=(
-            jax.ShapeDtypeStruct((nv, rows) + tile, jnp.float32),
-            jax.ShapeDtypeStruct((count,) + tile, jnp.float32),
-        ),
-        in_specs=[smem, vmem, vmem, vmem],
-        out_specs=(vmem, vmem),
-        scratch_shapes=[
-            VMEM((rows, nn) + tile, jnp.float32),
-            VMEM((rows, nv) + tile, jnp.float32),
-        ],
-        name="local_sweeps",
-    )(scalars, diag, corrected, neighbours)
     share = cells // n
-    blocks = packed.reshape(count, n, share).transpose(1, 0, 2)
-    got = exchange(blocks, "span", False, 2)
-    solved = pl.pallas_call(
-        lambda *refs: solve_kernel(nv, *refs),
-        out_shape=jax.ShapeDtypeStruct((n, 2 * nv, share), jnp.float32),
-        in_specs=[vmem],
-        out_specs=vmem,
-        name="solve",
-    )(got)
-    back = exchange(solved, "span", False, 3)
-    incoming = back.transpose(1, 0, 2).reshape((2 * nv,) + tile)
     update = pl.pallas_call(
-        lambda *refs: final_kernel(nv, *refs),
+        lambda *refs: sweeps_kernel(nv, *refs),
         out_shape=jax.ShapeDtypeStruct((nv, rows) + tile, jnp.float32),
         in_specs=[smem, vmem, vmem, vmem],
         out_specs=vmem,
-        scratch_shapes=[VMEM((rows, nv) + tile, jnp.float32)],
-        name="final_sweeps",
-    )(scalars, diag, source, incoming)
+        scratch_shapes=[
+            VMEM((nv, rows) + tile, jnp.float32),
+            VMEM((rows, nn) + tile, jnp.float32),
+            VMEM((rows, nv) + tile, jnp.float32),
+            VMEM((count,) + tile, jnp.float32),
+            VMEM((n, count, share), jnp.float32),
+            VMEM((n, count, share), jnp.float32),
+            VMEM((n, 2 * nv, share), jnp.float32),
+            VMEM((n, 2 * nv, share), jnp.float32),
+            VMEM((2 * nv,) + tile, jnp.float32),
+        ]
+        + semaphores("span", 2),
+        compiler_params=pltpu.CompilerParams(collective_id=1, has_side_effects=True),
+        name="sweeps",
+    )(scalars, diag, corrected, neighbours)
     return jnp.moveaxis(update.reshape(nv, rows, axial, width), 1, 2)
 
 

time: 81.8 us -> 55.3 us (0.68)
  Pallas kernels: 48.1 us -> 37.2 us
  other arithmetic: 13.8 us -> 3.04 us
  local copies, waits for them, and re-layouts: 17.4 us -> 13.6 us
    pallas_call x7 -> x2, Pallas kernels: 48.1 us -> 37.2 us  [the longest x1 21.8 us: body(): pl.pallas_call(lambda *refs: sweeps_kernel(nv, *refs), out_shape=jax.Shap...]
    add x1 -> x0, other arithmetic: 5.94 us -> none  [total(): result = result + term]
    another operation x4 -> x0, other arithmetic: 5.73 us -> none  [the longest x2 5.69 us: corrections(): jnp.stack([field[:, :width] * turn_cos[q] - field[:, width:] * turn_sin[q...]
    pallas_call x2 -> x0, local copies, waits for them, and re-layouts: 3.26 us -> none  [the longest x1 1.79 us: body(): pl.pallas_call(lambda *refs: local_kernel(nv, *refs), out_shape=(jax.Shap...]
    squeeze x0 -> x2, local copies, waits for them, and re-layouts: none -> 2.42 us  [the longest x1 1.72 us: corrections(): lax.dynamic_index_in_dim(jnp.asarray(tables(n, width, harmonics)), me, 0,...]
    slice x6 -> x0, local copies, waits for them, and re-layouts: 2.04 us -> none  [the longest x1 0.72 us: edges_of(): lax.dynamic_index_in_dim(gathered, device, 0, keepdims=False)[flat_rows:]]
    reduce_sum x1 -> x0, other arithmetic: 1 us -> none  [corrections(): correction = received.sum(axis=0).reshape(2, nv, rows, width)]
    scatter-add x2, other arithmetic: 0.02 us -> 0.86 us  [body(): residual.at[:, 0].add(correction[0]).at[:, -1].add(correction[1])]
where the time goes in v2:
time: 55.3 us; the launch traced here: 54.9 us
  Pallas kernels  37.2 us (67%)
  local copies, waits for them, and re-layouts  13.6 us (25%)
  other arithmetic  3.04 us (5%)
  matrix products  0.9 us (2%)
    pallas_call x1, Pallas kernels, body(): pl.pallas_call(lambda *refs: sweeps_kernel(nv, *refs), out_shape=jax.Shap...  21.8 us
    pallas_call x1, Pallas kernels, corrections(): pl.pallas_call(lambda *refs: spectral_kernel(nv, rows, *refs), out_shape=...  15.4 us
    reshape x3, local copies, waits for them, and re-layouts, by_row(): return jnp.moveaxis(field, -2, -3).reshape((-1, rows) + tile)  3.08 us
    unnamed x15, local copies, waits for them, and re-layouts  2.53 us
    transpose x3, local copies, waits for them, and re-layouts, by_row(): return jnp.moveaxis(field, -2, -3).reshape((-1, rows) + tile)  1.79 us
    squeeze x1, local copies, waits for them, and re-layouts, corrections(): lax.dynamic_index_in_dim(jnp.asarray(tables(n, width, harmonics)), me, 0,...  1.72 us
    reshape x2, local copies, waits for them, and re-layouts, body(): return jnp.moveaxis(update.reshape(nv, rows, axial, width), 1, 2)  1.69 us

profile of v2, /device:TPU:0, one launch (start us, length us, event | category | flops | bytes accessed | tf_op | source)
XLA Modules:
  0.0 54.9 jit_solution(11798905159176366910)
XLA Ops:
  0.0 0.9 %copy.37 = f32[5,4,8,256]{3,2,1,0:T(8,128)S(1)} copy(f32[5,4,8,256]{3,2,1,0:T(8,128)} %param.13) | data formatting | bytes 327680
  0.9 0.7 %reshape.131.refs_0_ = f32[150]{0:T(256)} reshape(f32[6,5,5]{2,1,0:T(8,128)S(1)} %copy.18) | data formatting | bytes 1200 | tf_op jit(solution)/shard_map/reshape | solution.py:388
  1.6 1.5 %copy.19 = f32[5,5,8,4,256]{4,3,2,1,0:T(4,128)S(1)} copy(f32[5,5,8,4,256]{4,2,3,1,0:T(8,128)} %bitcast.47) | data formatting | bytes 1638400 | tf_op jit(solution)/shard_map/transpose | solution.py:372
  3.1 1.2 %reshape.132.refs_1_ = f32[25,8,8,128]{3,2,1,0:T(8,128)} reshape(f32[5,5,8,4,256]{4,3,2,1,0:T(4,128)S(1)} %copy.19) | data formatting | bytes 1638400 | tf_op jit(solution)/shard_map/reshape | solution.py:372
  4.4 0.7 %fusion.3 = (f32[4]{0:T(128)S(1)}, f32[4]{0:T(128)S(1)}) fusion(f32[4,4]{1,0:T(4,128)} %constant.106.clone, s32[]{:T(128)S(6)} %select_n.22, f32[4,4]{1,0:T(4,128)} %constant.107.clone), kind=kLoop, calls=%fused_computation.26 | loop fusion | bytes 68 | tf_op jit(solution)/shard_map/jit(dynamic_index_in_dim)/squeeze | solution.py:315
  5.1 0.6 %pad_maximum_fusion.3.refs_0_ = f32[8]{0:T(128)} fusion(f32[4]{0:T(128)S(1)} %get-tuple-element.44, f32[4]{0:T(128)S(1)} %get-tuple-element.43), kind=kLoop, calls=%fused_computation.29 | loop fusion | flops 8 | bytes 64 | tf_op jit(solution)/shard_map/concatenate | solution.py:345
  6.2 0.6 %pad_maximum_fusion.refs_1_ = f32[88,256]{1,0:T(8,128)} fusion(f32[8,256]{1,0:T(8,128)S(1)} %reshape.135, f32[80,256]{1,0:T(8,128)S(1)} %bitcast.48), kind=kLoop, calls=%fused_computation.10 | loop fusion | flops 22528 | bytes 180224 | tf_op jit(solution)/shard_map/concatenate | solution.py:346
  6.9 1.7 %dynamic-slice_bitcast_fusion.refs_2_ = f32[2,256,128]{2,1,0:T(8,128)} fusion(f32[4,2,256,128]{3,2,1,0:T(8,128)} %constant.108.clone, s32[]{:T(128)S(6)} %select_n.22), kind=kLoop, calls=%fused_computation.3 | loop fusion | bytes 524292 | tf_op jit(solution)/shard_map/jit(dynamic_index_in_dim)/squeeze | solution.py:317
  8.8 0.9 %convolution_bitcast_fusion.refs_3_ = f32[100,128]{1,0:T(8,128)} fusion(f32[100,512]{1,0:T(8,128)S(1)} %reshape.136, s32[128]{0:T(128)S(1)} %multiply_add_fusion), kind=kOutput, calls=%fused_computation | convolution fusion | flops 78708736 | bytes 256512 | tf_op jit(solution)/shard_map/dot_general | solution.py:321
  9.7 0.6 %copy-done.5 = s32[2]{0:T(128)S(1)} copy-done((s32[2]{0:T(128)S(1)}, s32[2]{0:T(128)}, u32[]{:S(2)}) %copy-start.5) | copy-done | bytes 32
  10.3 0.6 %compare_select_fusion.1.refs_4_ = f32[2,128]{1,0:T(2,128)} fusion(f32[128]{0:T(128)S(1)} %fusion.5, s32[128]{0:T(128)S(1)} %multiply_add_fusion, s32[2]{0:T(128)S(1)} %copy-done.5), kind=kLoop, calls=%fused_computation.21 | loop fusion | flops 512 | bytes 2056 | tf_op jit(solution)/shard_map/mul | solution.py:324
  11.0 15.4 %spectral.1 = (f32[80,256]{1,0:T(8,128)}, f32[4,8,256]{2,1,0:T(8,128)}) custom-call(f32[8]{0:T(128)} %pad_maximum_fusion.3.refs_0_, f32[88,256]{1,0:T(8,128)} %pad_maximum_fusion.refs_1_, f32[2,256,128]{2,1,0:T(8,128)} %dynamic-slice_bitcast_fusion.refs_2_, f32[100,128]{1,0:T(8,128)} %convolution_bitcast_fusion.refs_3_, f32[2,128]{1,0:T(2,128)} %compare_select_fusion.1.refs_4_), custom_call_target="tpu_custom_call" | custom-call | tf_op jit(solution)/shard_map/spectral/pallas_call | solution.py:328
  26.4 0.9 %fusion.2 = f32[5,4,8,256]{3,2,1,0:T(8,128)S(1)} fusion(f32[5,4,8,256]{3,2,1,0:T(8,128)S(1)} %copy.37, f32[80,256]{1,0:T(8,128)} %get-tuple-element.31), kind=kLoop, calls=%fused_computation.16 | loop fusion | flops 10240 | bytes 122880 | tf_op jit(solution)/shard_map/scatter-add | solution.py:376
  27.3 0.7 %reshape.139.refs_2_ = f32[5,8,8,128]{3,2,1,0:T(8,128)} reshape(f32[5,8,4,256]{3,2,1,0:T(4,128)S(1)} %copy.25) | data formatting | bytes 327680 | tf_op jit(solution)/shard_map/reshape | solution.py:372
  28.1 0.7 %copy-done.4 = f32[4,8,256]{2,1,0:T(8,128)S(1)} copy-done((f32[4,8,256]{2,1,0:T(8,128)S(1)}, f32[4,8,256]{2,1,0:T(8,128)}, u32[]{:S(2)}) %copy-start.4) | copy-done | bytes 32792
  28.9 0.2 slice.115
  29.1 0.2 copy.27
  29.5 0.2 slice.111
  29.7 0.2 copy.26
  30.0 0.3 copy.28
  30.3 1.1 %reshape.140.refs_3_ = f32[20,8,8,128]{3,2,1,0:T(8,128)} reshape(f32[4,5,8,4,256]{4,3,2,1,0:T(4,128)S(1)} %copy.28) | data formatting | bytes 1310720 | tf_op jit(solution)/shard_map/reshape | solution.py:372
  31.4 21.8 %sweeps.1 = f32[5,8,8,128]{3,2,1,0:T(8,128)} custom-call(f32[150]{0:T(256)} %reshape.131.refs_0_, f32[25,8,8,128]{3,2,1,0:T(8,128)} %reshape.132.refs_1_, f32[5,8,8,128]{3,2,1,0:T(8,128)} %reshape.139.refs_2_, f32[20,8,8,128]{3,2,1,0:T(8,128)} %reshape.140.refs_3_), custom_call_target="tpu_custom_call" | custom-call | tf_op jit(solution)/shard_map/sweeps/pallas_call | solution.py:394
  53.3 1.0 %reshape.141 = f32[5,8,4,256]{3,2,1,0:T(4,128)S(1)} reshape(f32[5,8,8,128]{3,2,1,0:T(8,128)} %sweeps.1) | data formatting | bytes 327680 | tf_op jit(solution)/shard_map/reshape | solution.py:414
  54.2 0.7 %copy.33 = f32[5,8,4,256]{3,1,2,0:T(8,128)} copy(f32[5,8,4,256]{3,2,1,0:T(4,128)S(1)} %reshape.141) | data formatting | bytes 327680 | tf_op jit(solution)/shard_map/reshape | solution.py:414
  (34 shorter events, 1.2 us)
Async XLA Ops:
  0.0 0.9 %copy-start.3 = (f32[6,5,5]{2,0,1:T(8,128)S(1)}, f32[6,5,5]{2,0,1:T(8,128)}, u32[]{:S(2)}) copy-start(f32[6,5,5]{2,0,1:T(8,128)} %param.16) | copy-start | bytes 1804
  3.1 2.6 %copy-start = (f32[5,4,8,256]{3,2,1,0:T(8,128)S(1)}, f32[5,4,8,256]{3,2,1,0:T(8,128)}, u32[]{:S(2)}) copy-start(f32[5,4,8,256]{3,2,1,0:T(8,128)} %param.15) | copy-start | bytes 491524
  6.9 1.7 %copy-start.1 = (f32[2,2,512,5,5]{2,1,4,3,0:T(2,128)S(1)}, f32[2,2,512,5,5]{2,1,4,3,0:T(2,128)}, u32[]{:S(2)}) copy-start(f32[2,2,512,5,5]{2,1,4,3,0:T(2,128)} %param.17) | copy-start | bytes 614404
  9.7 0.7 %copy-start.5 = (s32[2]{0:T(128)S(1)}, s32[2]{0:T(128)}, u32[]{:S(2)}) copy-start(s32[2]{0:T(128)} %param.18) | copy-start | bytes 28
  26.3 0.9 %copy-start.2 = (f32[80,256]{1,0:T(8,128)S(1)}, f32[80,256]{1,0:T(8,128)}, u32[]{:S(2)}) copy-start(f32[80,256]{1,0:T(8,128)} %get-tuple-element.31) | copy-start | bytes 245764
  28.1 0.8 %copy-start.4 = (f32[4,8,256]{2,1,0:T(8,128)S(1)}, f32[4,8,256]{2,1,0:T(8,128)}, u32[]{:S(2)}) copy-start(f32[4,8,256]{2,1,0:T(8,128)} %get-tuple-element.32) | copy-start | bytes 98308

commit v3 on v2

--- a/solution.py
+++ b/solution.py
@@ -200,15 +200,34 @@
 
 
 def spectral_kernel(
-    nv, rows, turn, x_ref, table, picked, factor, out, edges, got, parts, landed, s0, r0, s1, r1
+    nv, rows, turns, cutoffs, x_ref, all_tables, entries, out, edges,
+    got, parts, landed, table, picked, fetched, s0, r0, s1, r1
 ):
     n = lax.axis_size("pitch")
     me = lax.axis_index("pitch")
     flat = 2 * nv * rows
     greet("pitch")
+    fetch = pltpu.make_async_copy(all_tables.at[me], table, fetched)
+    fetch.start()
     got[me] = x_ref[...]
+    turn = [turns[part * n * n + me * n + q] for part in range(2) for q in range(n)]
+    harmonics = entries.shape[1]
+    own = harmonics // n
+    points = n * x_ref.shape[1]
+    chosen = lax.broadcasted_iota(jnp.int32, (harmonics, own), 0) == (
+        n * lax.broadcasted_iota(jnp.int32, (harmonics, own), 1) + me
+    )
+    picked[...] = jnp.dot(
+        entries[...],
+        jnp.where(chosen, 1.0, 0.0).astype(jnp.float32),
+        precision=highest,
+        preferred_element_type=jnp.float32,
+    )
+    mine = n * lax.broadcasted_iota(jnp.int32, (1, own), 1) + me
+    weights = jnp.where(mine == 0, 1.0, 2.0).astype(jnp.float32) / points
     greeted("pitch")
     wait_all(start_exchange(x_ref, got, s0, r0, "pitch", True))
+    fetch.wait()
     edges[...] = got[:, flat:, :]
     waves = total([got[q, :flat, :] * turn[q] for q in range(n)])
     waves_imag = -total([got[q, :flat, :] * turn[n + q] for q in range(n)])
@@ -220,7 +239,7 @@
     imag_part = with_cos[flat:] - with_sin[:flat]
     out_real, out_imag = [], []
     for q in range(2):
-        weight = factor[q:q + 1, :]
+        weight = jnp.where(mine < cutoffs[q], weights, 0.0)
         sr = [real_part[(q * nv + j) * rows:(q * nv + j + 1) * rows] for j in range(nv)]
         si = [imag_part[(q * nv + j) * rows:(q * nv + j + 1) * rows] for j in range(nv)]
         for i in range(nv):
@@ -312,16 +331,8 @@
     edge_rows = -(-edge_rows // 8) * 8
     edges = jnp.pad(edges, (0, edge_rows * width - edges.shape[0])).reshape(edge_rows, width)
     turn = 2.0 * np.pi * (np.arange(n)[:, None] * np.arange(n)[None, :] % n) / n
-    turn_cos = lax.dynamic_index_in_dim(jnp.asarray(np.cos(turn), jnp.float32), me, 0, keepdims=False)
-    turn_sin = lax.dynamic_index_in_dim(jnp.asarray(np.sin(turn), jnp.float32), me, 0, keepdims=False)
-    table = lax.dynamic_index_in_dim(jnp.asarray(tables(n, width, harmonics)), me, 0, keepdims=False)
-    mine = n * jnp.arange(own, dtype=jnp.int32) + me
-    chosen = (jnp.arange(harmonics, dtype=jnp.int32)[:, None] == mine[None, :]).astype(jnp.float32)
-    by_entry = characteristic.transpose(3, 4, 0, 1, 2).reshape(-1, harmonics)
-    picked = jnp.dot(by_entry, chosen, precision=highest)
-    kept = (mine[None, :] < cutoffs[:, None]).astype(jnp.float32)
-    weight = jnp.where(mine == 0, 1.0, 2.0).astype(jnp.float32) / points
-    factor = kept * weight[None, :]
+    turns = jnp.asarray(np.concatenate([np.cos(turn), np.sin(turn)]).reshape(-1), jnp.float32)
+    entries = characteristic.transpose(3, 4, 0, 1, 2).reshape(-1, harmonics)
     smem = pl.BlockSpec(memory_space=SMEM)
     vmem = pl.BlockSpec(memory_space=VMEM)
     total_rows = flat_rows + edge_rows
@@ -331,22 +342,25 @@
             jax.ShapeDtypeStruct((flat_rows, width), jnp.float32),
             jax.ShapeDtypeStruct((n, edge_rows, width), jnp.float32),
         ),
-        in_specs=[smem, vmem, vmem, vmem, vmem],
+        in_specs=[smem, smem, vmem, pl.BlockSpec(memory_space=pl.ANY), vmem],
         out_specs=(vmem, vmem),
         scratch_shapes=[
             VMEM((n, total_rows, width), jnp.float32),
             VMEM((n, flat_rows, width), jnp.float32),
             VMEM((n, flat_rows, width), jnp.float32),
+            VMEM((2, width, own), jnp.float32),
+            VMEM((entries.shape[0], own), jnp.float32),
+            pltpu.SemaphoreType.DMA,
         ]
         + semaphores("pitch", 2),
         compiler_params=pltpu.CompilerParams(collective_id=0, has_side_effects=True),
         name="spectral",
     )(
-        jnp.concatenate([turn_cos, turn_sin]),
+        turns,
+        cutoffs,
         jnp.concatenate([planes, edges]),
-        table,
-        picked,
-        factor,
+        jnp.asarray(tables(n, width, harmonics)),
+        entries,
     )
     edge_shape = (2,) + prior.shape[:-1]
     count = int(np.prod(edge_shape))

time: 55.3 us -> 51 us (0.922)
  local copies, waits for them, and re-layouts: 13.6 us -> 11.5 us
  other arithmetic: 3.04 us -> 1.71 us
  matrix products: 0.9 us -> 0 us
    squeeze x2 -> x0, local copies, waits for them, and re-layouts: 2.42 us -> none  [the longest x1 1.72 us: corrections(): lax.dynamic_index_in_dim(jnp.asarray(tables(n, width, harmonics)), me, 0,...]
    dot_general x1 -> x0, matrix products: 0.9 us -> none  [corrections(): picked = jnp.dot(by_entry, chosen, precision=highest)]
    reshape x1, local copies, waits for them, and re-layouts: 0.14 us -> 0.82 us  [corrections(): entries = characteristic.transpose(3, 4, 0, 1, 2).reshape(-1, harmonics)]
    mul x1 -> x0, other arithmetic: 0.64 us -> none  [corrections(): factor = kept * weight[None, :]]
    concatenate x1 -> x0, other arithmetic: 0.6 us -> none  [corrections(): jnp.concatenate([turn_cos, turn_sin])]
    unnamed x15 -> x13, local copies, waits for them, and re-layouts: 2.53 us -> 2.18 us
where the time goes in v3:
time: 51 us; the launch traced here: 50.6 us
  Pallas kernels  37.2 us (73%)
  local copies, waits for them, and re-layouts  11.5 us (23%)
  other arithmetic  1.71 us (3%)
    pallas_call x1, Pallas kernels, body(): pl.pallas_call(lambda *refs: sweeps_kernel(nv, *refs), out_shape=jax.Shap...  21.8 us
    pallas_call x1, Pallas kernels, corrections(): pl.pallas_call(lambda *refs: spectral_kernel(nv, rows, *refs), out_shape=...  15.4 us
    reshape x3, local copies, waits for them, and re-layouts, by_row(): return jnp.moveaxis(field, -2, -3).reshape((-1, rows) + tile)  3.07 us
    unnamed x13, local copies, waits for them, and re-layouts  2.18 us
    transpose x3, local copies, waits for them, and re-layouts, by_row(): return jnp.moveaxis(field, -2, -3).reshape((-1, rows) + tile)  1.79 us
    reshape x2, local copies, waits for them, and re-layouts, body(): return jnp.moveaxis(update.reshape(nv, rows, axial, width), 1, 2)  1.69 us

profile of v3, /device:TPU:0, one launch (start us, length us, event | category | flops | bytes accessed | tf_op | source)
XLA Modules:
  0.0 50.6 jit_solution(9699590126798344784)
XLA Ops:
  0.0 0.9 %copy.37 = f32[5,4,8,256]{3,2,1,0:T(8,128)S(1)} copy(f32[5,4,8,256]{3,2,1,0:T(8,128)} %param.12) | data formatting | bytes 327680
  0.9 0.7 %reshape.120.refs_0_ = f32[150]{0:T(256)} reshape(f32[6,5,5]{2,1,0:T(8,128)S(1)} %copy.18) | data formatting | bytes 1200 | tf_op jit(solution)/shard_map/reshape | solution.py:402
  1.6 1.5 %copy.19 = f32[5,5,8,4,256]{4,3,2,1,0:T(4,128)S(1)} copy(f32[5,5,8,4,256]{4,2,3,1,0:T(8,128)} %bitcast.38) | data formatting | bytes 1638400 | tf_op jit(solution)/shard_map/transpose | solution.py:386
  3.1 1.2 %reshape.121.refs_1_ = f32[25,8,8,128]{3,2,1,0:T(8,128)} reshape(f32[5,5,8,4,256]{4,3,2,1,0:T(4,128)S(1)} %copy.19) | data formatting | bytes 1638400 | tf_op jit(solution)/shard_map/reshape | solution.py:386
  4.3 0.2 fusion.4
  4.5 0.2 copy.31
  4.9 0.6 %pad_maximum_fusion.refs_2_ = f32[88,256]{1,0:T(8,128)} fusion(f32[8,256]{1,0:T(8,128)S(1)} %reshape.124, f32[80,256]{1,0:T(8,128)S(1)} %bitcast.39), kind=kLoop, calls=%fused_computation.6 | loop fusion | flops 22528 | bytes 180224 | tf_op jit(solution)/shard_map/concatenate | solution.py:361
  5.5 0.3 copy-done.1
  5.9 0.8 %reshape.125.refs_4_ = f32[100,512]{1,0:T(8,128)} reshape(f32[5,5,2,2,512]{4,3,2,1,0:T(2,128)S(1)} %copy.22) | data formatting | bytes 409600 | tf_op jit(solution)/shard_map/reshape | solution.py:335
  6.7 15.4 %spectral.1 = (f32[80,256]{1,0:T(8,128)}, f32[4,8,256]{2,1,0:T(8,128)}) custom-call(f32[32]{0:T(128)} %constant.84.clone.refs_0_, s32[2]{0:T(128)} %refs_1_.1, f32[88,256]{1,0:T(8,128)} %pad_maximum_fusion.refs_2_, f32[4,2,256,128]{3,2,1,0:T(8,128)} %constant.85.clone.refs_3_, f32[100,512]{1,0:T(8,128)} %reshape.125.refs_4_), custom_call_target="tpu_custom_call" | custom-call | tf_op jit(solution)/shard_map/spectral/pallas_call | solution.py:339
  22.1 0.9 %fusion.1 = f32[5,4,8,256]{3,2,1,0:T(8,128)S(1)} fusion(f32[5,4,8,256]{3,2,1,0:T(8,128)S(1)} %copy.37, f32[80,256]{1,0:T(8,128)} %get-tuple-element.31), kind=kLoop, calls=%fused_computation.12 | loop fusion | flops 10240 | bytes 122880 | tf_op jit(solution)/shard_map/scatter-add | solution.py:390
  23.0 0.7 %reshape.128.refs_2_ = f32[5,8,8,128]{3,2,1,0:T(8,128)} reshape(f32[5,8,4,256]{3,2,1,0:T(4,128)S(1)} %copy.25) | data formatting | bytes 327680 | tf_op jit(solution)/shard_map/reshape | solution.py:386
  23.8 0.1 fusion.2
  24.0 0.7 %copy-done.4 = f32[4,8,256]{2,1,0:T(8,128)S(1)} copy-done((f32[4,8,256]{2,1,0:T(8,128)S(1)}, f32[4,8,256]{2,1,0:T(8,128)}, u32[]{:S(2)}) %copy-start.4) | copy-done | bytes 32792
  24.7 0.2 slice.111
  24.9 0.2 copy.26
  25.1 0.2 slice.115
  25.3 0.2 copy.27
  25.5 0.1 maximum_bitcast_fusion.1
  25.7 0.3 copy.28
  26.0 1.1 %reshape.129.refs_3_ = f32[20,8,8,128]{3,2,1,0:T(8,128)} reshape(f32[4,5,8,4,256]{4,3,2,1,0:T(4,128)S(1)} %copy.28) | data formatting | bytes 1310720 | tf_op jit(solution)/shard_map/reshape | solution.py:386
  27.1 21.8 %sweeps.1 = f32[5,8,8,128]{3,2,1,0:T(8,128)} custom-call(f32[150]{0:T(256)} %reshape.120.refs_0_, f32[25,8,8,128]{3,2,1,0:T(8,128)} %reshape.121.refs_1_, f32[5,8,8,128]{3,2,1,0:T(8,128)} %reshape.128.refs_2_, f32[20,8,8,128]{3,2,1,0:T(8,128)} %reshape.129.refs_3_), custom_call_target="tpu_custom_call" | custom-call | tf_op jit(solution)/shard_map/sweeps/pallas_call | solution.py:408
  48.9 1.0 %reshape.130 = f32[5,8,4,256]{3,2,1,0:T(4,128)S(1)} reshape(f32[5,8,8,128]{3,2,1,0:T(8,128)} %sweeps.1) | data formatting | bytes 327680 | tf_op jit(solution)/shard_map/reshape | solution.py:428
  49.9 0.7 %copy.33 = f32[5,8,4,256]{3,1,2,0:T(8,128)} copy(f32[5,8,4,256]{3,2,1,0:T(4,128)S(1)} %reshape.130) | data formatting | bytes 327680 | tf_op jit(solution)/shard_map/reshape | solution.py:428
  (24 shorter events, 0.4 us)
Async XLA Ops:
  0.0 0.9 %copy-start.3 = (f32[6,5,5]{2,0,1:T(8,128)S(1)}, f32[6,5,5]{2,0,1:T(8,128)}, u32[]{:S(2)}) copy-start(f32[6,5,5]{2,0,1:T(8,128)} %param.15) | copy-start | bytes 1804
  3.1 1.2 %copy-start = (f32[5,4,8,256]{3,2,1,0:T(8,128)S(1)}, f32[5,4,8,256]{3,2,1,0:T(8,128)}, u32[]{:S(2)}) copy-start(f32[5,4,8,256]{3,2,1,0:T(8,128)} %param.14) | copy-start | bytes 491524
  4.9 1.0 %copy-start.1 = (f32[2,2,512,5,5]{2,1,4,3,0:T(2,128)S(1)}, f32[2,2,512,5,5]{2,1,4,3,0:T(2,128)}, u32[]{:S(2)}) copy-start(f32[2,2,512,5,5]{2,1,4,3,0:T(2,128)} %param.16) | copy-start | bytes 614404
  22.1 0.9 %copy-start.2 = (f32[80,256]{1,0:T(8,128)S(1)}, f32[80,256]{1,0:T(8,128)}, u32[]{:S(2)}) copy-start(f32[80,256]{1,0:T(8,128)} %get-tuple-element.31) | copy-start | bytes 245764
  23.9 0.8 %copy-start.4 = (f32[4,8,256]{2,1,0:T(8,128)S(1)}, f32[4,8,256]{2,1,0:T(8,128)}, u32[]{:S(2)}) copy-start(f32[4,8,256]{2,1,0:T(8,128)} %get-tuple-element.32) | copy-start | bytes 98308

commit v4 on v3

--- a/solution.py
+++ b/solution.py
@@ -33,7 +33,7 @@
     n = lax.axis_size(axis)
     me = lax.axis_index(axis)
     copies = []
-    for step in range(1, n):
+    for step in sorted(range(1, n), key=lambda step: -min(step, n - step)):
         to = lax.rem(me + step, n)
         copy = pltpu.make_async_remote_copy(
             src_ref=source if gather else source.at[to],

time: 51 us -> 51.5 us (level)
    pallas_call x1, Pallas kernels: 15.4 us -> 16.8 us  [corrections(): pl.pallas_call(lambda *refs: spectral_kernel(nv, rows, *refs), out_shape=...]
    pallas_call x1, Pallas kernels: 21.8 us -> 20.9 us  [body(): pl.pallas_call(lambda *refs: sweeps_kernel(nv, *refs), out_shape=jax.Shap...]
where the time goes in v4:
time: 51.5 us; the launch traced here: 51.1 us
  Pallas kernels  37.7 us (73%)
  local copies, waits for them, and re-layouts  11.5 us (22%)
  other arithmetic  1.71 us (3%)
    pallas_call x1, Pallas kernels, body(): pl.pallas_call(lambda *refs: sweeps_kernel(nv, *refs), out_shape=jax.Shap...  20.9 us
    pallas_call x1, Pallas kernels, corrections(): pl.pallas_call(lambda *refs: spectral_kernel(nv, rows, *refs), out_shape=...  16.8 us
    reshape x3, local copies, waits for them, and re-layouts, by_row(): return jnp.moveaxis(field, -2, -3).reshape((-1, rows) + tile)  3.07 us
    unnamed x13, local copies, waits for them, and re-layouts  2.18 us
    transpose x3, local copies, waits for them, and re-layouts, by_row(): return jnp.moveaxis(field, -2, -3).reshape((-1, rows) + tile)  1.79 us
    reshape x2, local copies, waits for them, and re-layouts, body(): return jnp.moveaxis(update.reshape(nv, rows, axial, width), 1, 2)  1.69 us

profile of v4, /device:TPU:0, one launch (start us, length us, event | category | flops | bytes accessed | tf_op | source)
XLA Modules:
  0.0 51.1 jit_solution(3452745017591386446)
XLA Ops:
  0.0 0.9 %copy.37 = f32[5,4,8,256]{3,2,1,0:T(8,128)S(1)} copy(f32[5,4,8,256]{3,2,1,0:T(8,128)} %param.12) | data formatting | bytes 327680
  0.9 0.7 %reshape.120.refs_0_ = f32[150]{0:T(256)} reshape(f32[6,5,5]{2,1,0:T(8,128)S(1)} %copy.18) | data formatting | bytes 1200 | tf_op jit(solution)/shard_map/reshape | solution.py:402
  1.6 1.5 %copy.19 = f32[5,5,8,4,256]{4,3,2,1,0:T(4,128)S(1)} copy(f32[5,5,8,4,256]{4,2,3,1,0:T(8,128)} %bitcast.38) | data formatting | bytes 1638400 | tf_op jit(solution)/shard_map/transpose | solution.py:386
  3.1 1.2 %reshape.121.refs_1_ = f32[25,8,8,128]{3,2,1,0:T(8,128)} reshape(f32[5,5,8,4,256]{4,3,2,1,0:T(4,128)S(1)} %copy.19) | data formatting | bytes 1638400 | tf_op jit(solution)/shard_map/reshape | solution.py:386
  4.3 0.2 fusion.4
  4.5 0.2 copy.31
  4.9 0.6 %pad_maximum_fusion.refs_2_ = f32[88,256]{1,0:T(8,128)} fusion(f32[8,256]{1,0:T(8,128)S(1)} %reshape.124, f32[80,256]{1,0:T(8,128)S(1)} %bitcast.39), kind=kLoop, calls=%fused_computation.6 | loop fusion | flops 22528 | bytes 180224 | tf_op jit(solution)/shard_map/concatenate | solution.py:361
  5.5 0.3 copy-done.1
  5.9 0.8 %reshape.125.refs_4_ = f32[100,512]{1,0:T(8,128)} reshape(f32[5,5,2,2,512]{4,3,2,1,0:T(2,128)S(1)} %copy.22) | data formatting | bytes 409600 | tf_op jit(solution)/shard_map/reshape | solution.py:335
  6.7 16.8 %spectral.1 = (f32[80,256]{1,0:T(8,128)}, f32[4,8,256]{2,1,0:T(8,128)}) custom-call(f32[32]{0:T(128)} %constant.84.clone.refs_0_, s32[2]{0:T(128)} %refs_1_.1, f32[88,256]{1,0:T(8,128)} %pad_maximum_fusion.refs_2_, f32[4,2,256,128]{3,2,1,0:T(8,128)} %constant.85.clone.refs_3_, f32[100,512]{1,0:T(8,128)} %reshape.125.refs_4_), custom_call_target="tpu_custom_call" | custom-call | tf_op jit(solution)/shard_map/spectral/pallas_call | solution.py:339
  23.5 0.9 %fusion.1 = f32[5,4,8,256]{3,2,1,0:T(8,128)S(1)} fusion(f32[5,4,8,256]{3,2,1,0:T(8,128)S(1)} %copy.37, f32[80,256]{1,0:T(8,128)} %get-tuple-element.31), kind=kLoop, calls=%fused_computation.12 | loop fusion | flops 10240 | bytes 122880 | tf_op jit(solution)/shard_map/scatter-add | solution.py:390
  24.5 0.7 %reshape.128.refs_2_ = f32[5,8,8,128]{3,2,1,0:T(8,128)} reshape(f32[5,8,4,256]{3,2,1,0:T(4,128)S(1)} %copy.25) | data formatting | bytes 327680 | tf_op jit(solution)/shard_map/reshape | solution.py:386
  25.3 0.1 fusion.2
  25.4 0.7 %copy-done.4 = f32[4,8,256]{2,1,0:T(8,128)S(1)} copy-done((f32[4,8,256]{2,1,0:T(8,128)S(1)}, f32[4,8,256]{2,1,0:T(8,128)}, u32[]{:S(2)}) %copy-start.4) | copy-done | bytes 32792
  26.2 0.2 slice.111
  26.4 0.2 copy.26
  26.6 0.2 slice.115
  26.8 0.2 copy.27
  27.0 0.1 maximum_bitcast_fusion.1
  27.1 0.3 copy.28
  27.4 1.1 %reshape.129.refs_3_ = f32[20,8,8,128]{3,2,1,0:T(8,128)} reshape(f32[4,5,8,4,256]{4,3,2,1,0:T(4,128)S(1)} %copy.28) | data formatting | bytes 1310720 | tf_op jit(solution)/shard_map/reshape | solution.py:386
  28.5 20.9 %sweeps.1 = f32[5,8,8,128]{3,2,1,0:T(8,128)} custom-call(f32[150]{0:T(256)} %reshape.120.refs_0_, f32[25,8,8,128]{3,2,1,0:T(8,128)} %reshape.121.refs_1_, f32[5,8,8,128]{3,2,1,0:T(8,128)} %reshape.128.refs_2_, f32[20,8,8,128]{3,2,1,0:T(8,128)} %reshape.129.refs_3_), custom_call_target="tpu_custom_call" | custom-call | tf_op jit(solution)/shard_map/sweeps/pallas_call | solution.py:408
  49.4 1.0 %reshape.130 = f32[5,8,4,256]{3,2,1,0:T(4,128)S(1)} reshape(f32[5,8,8,128]{3,2,1,0:T(8,128)} %sweeps.1) | data formatting | bytes 327680 | tf_op jit(solution)/shard_map/reshape | solution.py:428
  50.4 0.7 %copy.33 = f32[5,8,4,256]{3,1,2,0:T(8,128)} copy(f32[5,8,4,256]{3,2,1,0:T(4,128)S(1)} %reshape.130) | data formatting | bytes 327680 | tf_op jit(solution)/shard_map/reshape | solution.py:428
  (24 shorter events, 0.4 us)
Async XLA Ops:
  0.0 0.9 %copy-start.3 = (f32[6,5,5]{2,0,1:T(8,128)S(1)}, f32[6,5,5]{2,0,1:T(8,128)}, u32[]{:S(2)}) copy-start(f32[6,5,5]{2,0,1:T(8,128)} %param.15) | copy-start | bytes 1804
  3.1 1.2 %copy-start = (f32[5,4,8,256]{3,2,1,0:T(8,128)S(1)}, f32[5,4,8,256]{3,2,1,0:T(8,128)}, u32[]{:S(2)}) copy-start(f32[5,4,8,256]{3,2,1,0:T(8,128)} %param.14) | copy-start | bytes 491524
  4.9 1.0 %copy-start.1 = (f32[2,2,512,5,5]{2,1,4,3,0:T(2,128)S(1)}, f32[2,2,512,5,5]{2,1,4,3,0:T(2,128)}, u32[]{:S(2)}) copy-start(f32[2,2,512,5,5]{2,1,4,3,0:T(2,128)} %param.16) | copy-start | bytes 614404
  23.5 0.9 %copy-start.2 = (f32[80,256]{1,0:T(8,128)S(1)}, f32[80,256]{1,0:T(8,128)}, u32[]{:S(2)}) copy-start(f32[80,256]{1,0:T(8,128)} %get-tuple-element.31) | copy-start | bytes 245764
  25.4 0.8 %copy-start.4 = (f32[4,8,256]{2,1,0:T(8,128)S(1)}, f32[4,8,256]{2,1,0:T(8,128)}, u32[]{:S(2)}) copy-start(f32[4,8,256]{2,1,0:T(8,128)} %get-tuple-element.32) | copy-start | bytes 98308
